TPU v7x, 512 devices: a whole 4x4x16 slice. The times are simulated.
512 devices in a mesh: inline: 32 (over z, core), xline: 16 (over x, y).
Axes of the slice: x: 4, y: 4, z: 16, core: 2. Of those that a mesh axis runs over, the one named last changes fastest.
Arguments:
- probes: float32 [2, 512, 512, 128], P(None, 'inline', 'xline'), may hold values from -6 to 6
- diffusion: bfloat16 [3, 512, 512, 128], P(None, 'inline', 'xline'), may hold values from -1 to 1, as said below
- wavelet: float32 [41], replicated, may hold values from -1 to 1
Outputs:
- iterate: float32 [2, 512, 512, 128], P(None, 'inline', 'xline')
Inputs may be any that keep to these rules, and one draw needn't show every extreme that they name: `diffusion`: components 0 and 2 are positive; component 1 lies within nine tenths of the root of their product in magnitude.
All inputs are finite; a program needn't handle non-finite values.
Results may differ from a plain program's by a relative error of at most 0.0003.
Values may be sent and summed in bfloat16 or wider, within the bound.
No kernel may reach another device: no remote copies, remote signals or barrier semaphores. Data moves between devices by JAX's collectives and lax.ppermute only.
A program may use at most 64 MiB of HBM per device.

v0:
```python
import jax
import jax.numpy as jnp
from jax import lax
from jax.sharding import PartitionSpec as P

HALF = 20
PAIRS = 3


def shifted(value, axis, by):
    count = lax.axis_size(axis)
    pairs = [(i, i + by) for i in range(count) if 0 <= i + by < count]
    return lax.ppermute(value, axis, pairs)


def with_halo(block, sides, width):
    for axis, dim in sides:
        count = lax.axis_size(axis)
        forward = [(i, i + 1) for i in range(count - 1)]
        backward = [(target, source) for source, target in forward]
        low = lax.ppermute(
            lax.slice_in_dim(block, block.shape[dim] - width, None, axis=dim), axis, forward
        )
        high = lax.ppermute(lax.slice_in_dim(block, 0, width, axis=dim), axis, backward)
        block = jnp.concatenate([low, block, high], axis=dim)
    return block


def wavelet_matrix(wavelet, samples):
    offset = jnp.arange(samples)[None, :] - jnp.arange(samples)[:, None] + HALF
    onehot = (offset[:, :, None] == jnp.arange(2 * HALF + 1)[None, None, :]).astype(jnp.float32)
    return jnp.einsum("stk,k->st", onehot, wavelet, precision=lax.Precision.HIGHEST)


def apply_data(volume, matrices):
    shape = volume.shape
    trace_rows = volume.reshape(-1, shape[-1])
    for matrix in matrices:
        trace_rows = jnp.dot(trace_rows, matrix, precision=lax.Precision.HIGHEST)
    return trace_rows.reshape(shape)


def regularize(extended, tensor):
    middle = extended[:, :-1, :-1]
    step_in = extended[:, 1:, :-1] - middle
    step_x = extended[:, :-1, 1:] - middle
    flux_in = tensor[0] * step_in + tensor[1] * step_x
    flux_x = tensor[1] * step_in + tensor[2] * step_x
    return flux_in[:, :-1, 1:] - flux_in[:, 1:, 1:] + (flux_x[:, 1:, :-1] - flux_x[:, 1:, 1:])


def per_device(probes, diffusion, wavelet):
    samples = probes.shape[-1]
    wavelet_band = wavelet_matrix(wavelet, samples)
    matrices = (wavelet_band, wavelet_band.T)
    below_in = shifted(diffusion[:, -1:], "inline", 1)
    below_x = shifted(diffusion[:, :, -1:], "xline", 1)
    corner = jnp.zeros((3, 1, 1, samples), diffusion.dtype)
    top_row = jnp.concatenate([corner, below_in], axis=2)
    remainder = jnp.concatenate([below_x, diffusion], axis=2)
    tensor = jnp.concatenate([top_row, remainder], axis=1).astype(jnp.float32)
    result = probes
    for turn in range(2 * PAIRS):
        extended = with_halo(result, (("inline", 1), ("xline", 2)), 1)
        result = result - 0.25 * (apply_data(result, matrices) + regularize(extended, tensor))
    return result


def solution(mesh):
    return jax.shard_map(
        per_device,
        mesh=mesh,
        in_specs=(P(None, "inline", "xline", None), P(None, "inline", "xline", None), P()),
        out_specs=P(None, "inline", "xline", None),
        check_vma=False,
    )
```

profile of v0, /device:TPU:121, one launch (start us, length us, event | category | flops | bytes accessed | tf_op | source)
XLA Modules:
  0.0 129.3 jit_solution(10137773370787981052)
XLA Ops:
  0.8 5.3 %collective-permute-start = (bf16[3,1,32,128]{3,2,1,0:T(8,128)(2,1)S(1)}, bf16[3,1,32,128]{3,2,1,0:T(8,128)(2,1)S(1)}, u32[]{:S(2)}, u32[]{:S(2)}) collective-permute-start(bf16[3,1,32,128]{3,2,1,0:T(8,128)(2,1)S(1)} %slice.252), channel_id=1, source_target_pairs={{0,16},{16,32},{32,48},{48,64},{64,80},{80,96},{96,112},{112,128},... | collective-permute-start | bytes 73736 | tf_op jit(solution)/shard_map/ppermute | solution.py:13
  7.0 2.8 %collective-permute-start.1 = (bf16[3,16,1,128]{3,2,1,0:T(2,128)(2,1)S(1)}, bf16[3,16,1,128]{3,2,1,0:T(2,128)(2,1)S(1)}, u32[]{:S(2)}, u32[]{:S(2)}) collective-permute-start(bf16[3,16,1,128]{3,2,1,0:T(2,128)(2,1)S(1)} %slice.253), channel_id=1, source_target_pairs={{0,1},{1,2},{2,3},{3,4},{4,5},{5,6},{6,7},{7,8},{8,9},{9,10},{10,1... | collective-permute-start | bytes 36872 | tf_op jit(solution)/shard_map/ppermute | solution.py:13
  19.2 3.2 %collective-permute-start.4 = (f32[2,18,1,128]{3,2,1,0:T(1,128)S(1)}, f32[2,18,1,128]{3,2,1,0:T(1,128)S(1)}, u32[]{:S(2)}, u32[]{:S(2)}) collective-permute-start(f32[2,18,1,128]{3,2,1,0:T(1,128)S(1)} %get-tuple-element.31), channel_id=1, source_target_pairs={{0,1},{1,2},{2,3},{3,4},{4,5},{5,6},{6,7},{7,8},{8,9},{9,10},{10,1... | collective-permute-start | bytes 55304 | tf_op jit(solution)/shard_map/ppermute | solution.py:21
  24.6 4.4 %collective-permute-done.5 = f32[2,18,1,128]{3,2,1,0:T(1,128)S(1)} collective-permute-done((f32[2,18,1,128]{3,2,1,0:T(1,128)S(1)}, f32[2,18,1,128]{3,2,1,0:T(1,128)S(1)}, u32[]{:S(2)}, u32[]{:S(2)}) %collective-permute-start.5) | collective-permute-done | bytes 18464 | tf_op jit(solution)/shard_map/ppermute | solution.py:24
  29.6 5.8 %collective-permute-start.6 = (f32[2,1,32,128]{3,2,1,0:T(8,128)S(1)}, f32[2,1,32,128]{3,2,1,0:T(8,128)S(1)}, u32[]{:S(2)}, u32[]{:S(2)}) collective-permute-start(f32[2,1,32,128]{3,2,1,0:T(8,128)S(1)} %get-tuple-element.40), channel_id=1, source_target_pairs={{0,16},{16,32},{32,48},{48,64},{64,80},{80,96},{96,112},{112,128},... | collective-permute-start | bytes 98312 | tf_op jit(solution)/shard_map/ppermute | solution.py:21
  37.9 3.9 %collective-permute-done.7 = f32[2,1,32,128]{3,2,1,0:T(8,128)S(1)} collective-permute-done((f32[2,1,32,128]{3,2,1,0:T(8,128)S(1)}, f32[2,1,32,128]{3,2,1,0:T(8,128)S(1)}, u32[]{:S(2)}, u32[]{:S(2)}) %collective-permute-start.7) | collective-permute-done | bytes 32800 | tf_op jit(solution)/shard_map/ppermute | solution.py:24
  44.4 3.4 %collective-permute-start.9 = (f32[2,18,1,128]{3,2,1,0:T(1,128)S(1)}, f32[2,18,1,128]{3,2,1,0:T(1,128)S(1)}, u32[]{:S(2)}, u32[]{:S(2)}) collective-permute-start(f32[2,18,1,128]{3,2,1,0:T(1,128)S(1)} %get-tuple-element.28), channel_id=1, source_target_pairs={{1,0},{2,1},{3,2},{4,3},{5,4},{6,5},{7,6},{8,7},{9,8},{10,9},{11,1... | collective-permute-start | bytes 55304 | tf_op jit(solution)/shard_map/ppermute | solution.py:24
  47.9 3.2 %collective-permute-done.9 = f32[2,18,1,128]{3,2,1,0:T(1,128)S(1)} collective-permute-done((f32[2,18,1,128]{3,2,1,0:T(1,128)S(1)}, f32[2,18,1,128]{3,2,1,0:T(1,128)S(1)}, u32[]{:S(2)}, u32[]{:S(2)}) %collective-permute-start.9) | collective-permute-done | bytes 18464 | tf_op jit(solution)/shard_map/ppermute | solution.py:24
  51.6 3.1 %collective-permute-start.10 = (f32[2,1,32,128]{3,2,1,0:T(8,128)S(1)}, f32[2,1,32,128]{3,2,1,0:T(8,128)S(1)}, u32[]{:S(2)}, u32[]{:S(2)}) collective-permute-start(f32[2,1,32,128]{3,2,1,0:T(8,128)S(1)} %get-tuple-element.38), channel_id=1, source_target_pairs={{0,16},{16,32},{32,48},{48,64},{64,80},{80,96},{96,112},{112,128},... | collective-permute-start | bytes 98312 | tf_op jit(solution)/shard_map/ppermute | solution.py:21
  57.2 3.9 %collective-permute-done.11 = f32[2,1,32,128]{3,2,1,0:T(8,128)S(1)} collective-permute-done((f32[2,1,32,128]{3,2,1,0:T(8,128)S(1)}, f32[2,1,32,128]{3,2,1,0:T(8,128)S(1)}, u32[]{:S(2)}, u32[]{:S(2)}) %collective-permute-start.11) | collective-permute-done | bytes 32800 | tf_op jit(solution)/shard_map/ppermute | solution.py:24
  63.6 3.4 %collective-permute-start.13 = (f32[2,18,1,128]{3,2,1,0:T(1,128)S(1)}, f32[2,18,1,128]{3,2,1,0:T(1,128)S(1)}, u32[]{:S(2)}, u32[]{:S(2)}) collective-permute-start(f32[2,18,1,128]{3,2,1,0:T(1,128)S(1)} %get-tuple-element.26), channel_id=1, source_target_pairs={{1,0},{2,1},{3,2},{4,3},{5,4},{6,5},{7,6},{8,7},{9,8},{10,9},{11,1... | collective-permute-start | bytes 55304 | tf_op jit(solution)/shard_map/ppermute | solution.py:24
  67.1 3.2 %collective-permute-done.13 = f32[2,18,1,128]{3,2,1,0:T(1,128)S(1)} collective-permute-done((f32[2,18,1,128]{3,2,1,0:T(1,128)S(1)}, f32[2,18,1,128]{3,2,1,0:T(1,128)S(1)}, u32[]{:S(2)}, u32[]{:S(2)}) %collective-permute-start.13) | collective-permute-done | bytes 18464 | tf_op jit(solution)/shard_map/ppermute | solution.py:24
  70.8 3.1 %collective-permute-start.14 = (f32[2,1,32,128]{3,2,1,0:T(8,128)S(1)}, f32[2,1,32,128]{3,2,1,0:T(8,128)S(1)}, u32[]{:S(2)}, u32[]{:S(2)}) collective-permute-start(f32[2,1,32,128]{3,2,1,0:T(8,128)S(1)} %get-tuple-element.36), channel_id=1, source_target_pairs={{0,16},{16,32},{32,48},{48,64},{64,80},{80,96},{96,112},{112,128},... | collective-permute-start | bytes 98312 | tf_op jit(solution)/shard_map/ppermute | solution.py:21
  76.4 3.9 %collective-permute-done.15 = f32[2,1,32,128]{3,2,1,0:T(8,128)S(1)} collective-permute-done((f32[2,1,32,128]{3,2,1,0:T(8,128)S(1)}, f32[2,1,32,128]{3,2,1,0:T(8,128)S(1)}, u32[]{:S(2)}, u32[]{:S(2)}) %collective-permute-start.15) | collective-permute-done | bytes 32800 | tf_op jit(solution)/shard_map/ppermute | solution.py:24
  82.8 3.4 %collective-permute-start.17 = (f32[2,18,1,128]{3,2,1,0:T(1,128)S(1)}, f32[2,18,1,128]{3,2,1,0:T(1,128)S(1)}, u32[]{:S(2)}, u32[]{:S(2)}) collective-permute-start(f32[2,18,1,128]{3,2,1,0:T(1,128)S(1)} %get-tuple-element.24), channel_id=1, source_target_pairs={{1,0},{2,1},{3,2},{4,3},{5,4},{6,5},{7,6},{8,7},{9,8},{10,9},{11,1... | collective-permute-start | bytes 55304 | tf_op jit(solution)/shard_map/ppermute | solution.py:24
  86.3 3.1 %collective-permute-done.17 = f32[2,18,1,128]{3,2,1,0:T(1,128)S(1)} collective-permute-done((f32[2,18,1,128]{3,2,1,0:T(1,128)S(1)}, f32[2,18,1,128]{3,2,1,0:T(1,128)S(1)}, u32[]{:S(2)}, u32[]{:S(2)}) %collective-permute-start.17) | collective-permute-done | bytes 18464 | tf_op jit(solution)/shard_map/ppermute | solution.py:24
  90.0 3.1 %collective-permute-start.18 = (f32[2,1,32,128]{3,2,1,0:T(8,128)S(1)}, f32[2,1,32,128]{3,2,1,0:T(8,128)S(1)}, u32[]{:S(2)}, u32[]{:S(2)}) collective-permute-start(f32[2,1,32,128]{3,2,1,0:T(8,128)S(1)} %get-tuple-element.34), channel_id=1, source_target_pairs={{0,16},{16,32},{32,48},{48,64},{64,80},{80,96},{96,112},{112,128},... | collective-permute-start | bytes 98312 | tf_op jit(solution)/shard_map/ppermute | solution.py:21
  95.6 3.9 %collective-permute-done.19 = f32[2,1,32,128]{3,2,1,0:T(8,128)S(1)} collective-permute-done((f32[2,1,32,128]{3,2,1,0:T(8,128)S(1)}, f32[2,1,32,128]{3,2,1,0:T(8,128)S(1)}, u32[]{:S(2)}, u32[]{:S(2)}) %collective-permute-start.19) | collective-permute-done | bytes 32800 | tf_op jit(solution)/shard_map/ppermute | solution.py:24
  102.2 3.4 %collective-permute-start.21 = (f32[2,18,1,128]{3,2,1,0:T(1,128)S(1)}, f32[2,18,1,128]{3,2,1,0:T(1,128)S(1)}, u32[]{:S(2)}, u32[]{:S(2)}) collective-permute-start(f32[2,18,1,128]{3,2,1,0:T(1,128)S(1)} %get-tuple-element.22), channel_id=1, source_target_pairs={{1,0},{2,1},{3,2},{4,3},{5,4},{6,5},{7,6},{8,7},{9,8},{10,9},{11,1... | collective-permute-start | bytes 55304 | tf_op jit(solution)/shard_map/ppermute | solution.py:24
  105.7 3.1 %collective-permute-done.21 = f32[2,18,1,128]{3,2,1,0:T(1,128)S(1)} collective-permute-done((f32[2,18,1,128]{3,2,1,0:T(1,128)S(1)}, f32[2,18,1,128]{3,2,1,0:T(1,128)S(1)}, u32[]{:S(2)}, u32[]{:S(2)}) %collective-permute-start.21) | collective-permute-done | bytes 18464 | tf_op jit(solution)/shard_map/ppermute | solution.py:24
  109.4 3.1 %collective-permute-start.22 = (f32[2,1,32,128]{3,2,1,0:T(8,128)S(1)}, f32[2,1,32,128]{3,2,1,0:T(8,128)S(1)}, u32[]{:S(2)}, u32[]{:S(2)}) collective-permute-start(f32[2,1,32,128]{3,2,1,0:T(8,128)S(1)} %get-tuple-element.32), channel_id=1, source_target_pairs={{0,16},{16,32},{32,48},{48,64},{64,80},{80,96},{96,112},{112,128},... | collective-permute-start | bytes 98312 | tf_op jit(solution)/shard_map/ppermute | solution.py:21
  115.0 3.9 %collective-permute-done.23 = f32[2,1,32,128]{3,2,1,0:T(8,128)S(1)} collective-permute-done((f32[2,1,32,128]{3,2,1,0:T(8,128)S(1)}, f32[2,1,32,128]{3,2,1,0:T(8,128)S(1)}, u32[]{:S(2)}, u32[]{:S(2)}) %collective-permute-start.23) | collective-permute-done | bytes 32800 | tf_op jit(solution)/shard_map/ppermute | solution.py:24
  121.4 3.4 %collective-permute-start.25 = (f32[2,18,1,128]{3,2,1,0:T(1,128)S(1)}, f32[2,18,1,128]{3,2,1,0:T(1,128)S(1)}, u32[]{:S(2)}, u32[]{:S(2)}) collective-permute-start(f32[2,18,1,128]{3,2,1,0:T(1,128)S(1)} %get-tuple-element.20), channel_id=1, source_target_pairs={{1,0},{2,1},{3,2},{4,3},{5,4},{6,5},{7,6},{8,7},{9,8},{10,9},{11,1... | collective-permute-start | bytes 55304 | tf_op jit(solution)/shard_map/ppermute | solution.py:24
  124.9 3.2 %collective-permute-done.25 = f32[2,18,1,128]{3,2,1,0:T(1,128)S(1)} collective-permute-done((f32[2,18,1,128]{3,2,1,0:T(1,128)S(1)}, f32[2,18,1,128]{3,2,1,0:T(1,128)S(1)}, u32[]{:S(2)}, u32[]{:S(2)}) %collective-permute-start.25) | collective-permute-done | bytes 18464 | tf_op jit(solution)/shard_map/ppermute | solution.py:24
  (85 shorter events, 42.7 us)
Async XLA Ops:
  0.8 17.9 %collective-permute-start = (bf16[3,1,32,128]{3,2,1,0:T(8,128)(2,1)S(1)}, bf16[3,1,32,128]{3,2,1,0:T(8,128)(2,1)S(1)}, u32[]{:S(2)}, u32[]{:S(2)}) collective-permute-start(bf16[3,1,32,128]{3,2,1,0:T(8,128)(2,1)S(1)} %slice.252), channel_id=1, source_target_pairs={{0,16},{16,32},{32,48},{48,64},{64,80},{80,96},{96,112},{112,128},... | collective-permute-start | bytes 73736 | tf_op jit(solution)/shard_map/ppermute | solution.py:13
  7.0 11.7 %collective-permute-start.1 = (bf16[3,16,1,128]{3,2,1,0:T(2,128)(2,1)S(1)}, bf16[3,16,1,128]{3,2,1,0:T(2,128)(2,1)S(1)}, u32[]{:S(2)}, u32[]{:S(2)}) collective-permute-start(bf16[3,16,1,128]{3,2,1,0:T(2,128)(2,1)S(1)} %slice.253), channel_id=1, source_target_pairs={{0,1},{1,2},{2,3},{3,4},{4,5},{5,6},{6,7},{7,8},{8,9},{9,10},{10,1... | collective-permute-start | bytes 36872 | tf_op jit(solution)/shard_map/ppermute | solution.py:13
  10.6 8.3 %collective-permute-start.2 = (f32[2,1,32,128]{3,2,1,0:T(8,128)S(1)}, f32[2,1,32,128]{3,2,1,0:T(8,128)S(1)}, u32[]{:S(2)}, u32[]{:S(2)}) collective-permute-start(f32[2,1,32,128]{3,2,1,0:T(8,128)S(1)} %get-tuple-element.43), channel_id=1, source_target_pairs={{0,16},{16,32},{32,48},{48,64},{64,80},{80,96},{96,112},{112,128},... | collective-permute-start | bytes 98312 | tf_op jit(solution)/shard_map/ppermute | solution.py:21
  12.8 6.4 %collective-permute-start.3 = (f32[2,1,32,128]{3,2,1,0:T(8,128)S(1)}, f32[2,1,32,128]{3,2,1,0:T(8,128)S(1)}, u32[]{:S(2)}, u32[]{:S(2)}) collective-permute-start(f32[2,1,32,128]{3,2,1,0:T(8,128)S(1)} %get-tuple-element.42), channel_id=1, source_target_pairs={{16,0},{32,16},{48,32},{64,48},{80,64},{96,80},{112,96},{128,112},... | collective-permute-start | bytes 98312 | tf_op jit(solution)/shard_map/ppermute | solution.py:24
  22.5 6.6 %collective-permute-start.5 = (f32[2,18,1,128]{3,2,1,0:T(1,128)S(1)}, f32[2,18,1,128]{3,2,1,0:T(1,128)S(1)}, u32[]{:S(2)}, u32[]{:S(2)}) collective-permute-start(f32[2,18,1,128]{3,2,1,0:T(1,128)S(1)} %get-tuple-element.30), channel_id=1, source_target_pairs={{1,0},{2,1},{3,2},{4,3},{5,4},{6,5},{7,6},{8,7},{9,8},{10,9},{11,1... | collective-permute-start | bytes 55304 | tf_op jit(solution)/shard_map/ppermute | solution.py:24
  29.6 8.3 %collective-permute-start.6 = (f32[2,1,32,128]{3,2,1,0:T(8,128)S(1)}, f32[2,1,32,128]{3,2,1,0:T(8,128)S(1)}, u32[]{:S(2)}, u32[]{:S(2)}) collective-permute-start(f32[2,1,32,128]{3,2,1,0:T(8,128)S(1)} %get-tuple-element.40), channel_id=1, source_target_pairs={{0,16},{16,32},{32,48},{48,64},{64,80},{80,96},{96,112},{112,128},... | collective-permute-start | bytes 98312 | tf_op jit(solution)/shard_map/ppermute | solution.py:21
  35.4 6.4 %collective-permute-start.7 = (f32[2,1,32,128]{3,2,1,0:T(8,128)S(1)}, f32[2,1,32,128]{3,2,1,0:T(8,128)S(1)}, u32[]{:S(2)}, u32[]{:S(2)}) collective-permute-start(f32[2,1,32,128]{3,2,1,0:T(8,128)S(1)} %get-tuple-element.41), channel_id=1, source_target_pairs={{16,0},{32,16},{48,32},{64,48},{80,64},{96,80},{112,96},{128,112},... | collective-permute-start | bytes 98312 | tf_op jit(solution)/shard_map/ppermute | solution.py:24
  41.9 5.9 %collective-permute-start.8 = (f32[2,18,1,128]{3,2,1,0:T(1,128)S(1)}, f32[2,18,1,128]{3,2,1,0:T(1,128)S(1)}, u32[]{:S(2)}, u32[]{:S(2)}) collective-permute-start(f32[2,18,1,128]{3,2,1,0:T(1,128)S(1)} %get-tuple-element.29), channel_id=1, source_target_pairs={{0,1},{1,2},{2,3},{3,4},{4,5},{5,6},{6,7},{7,8},{8,9},{9,10},{10,1... | collective-permute-start | bytes 55304 | tf_op jit(solution)/shard_map/ppermute | solution.py:21
  44.4 6.6 %collective-permute-start.9 = (f32[2,18,1,128]{3,2,1,0:T(1,128)S(1)}, f32[2,18,1,128]{3,2,1,0:T(1,128)S(1)}, u32[]{:S(2)}, u32[]{:S(2)}) collective-permute-start(f32[2,18,1,128]{3,2,1,0:T(1,128)S(1)} %get-tuple-element.28), channel_id=1, source_target_pairs={{1,0},{2,1},{3,2},{4,3},{5,4},{6,5},{7,6},{8,7},{9,8},{10,9},{11,1... | collective-permute-start | bytes 55304 | tf_op jit(solution)/shard_map/ppermute | solution.py:24
  54.7 6.4 %collective-permute-start.11 = (f32[2,1,32,128]{3,2,1,0:T(8,128)S(1)}, f32[2,1,32,128]{3,2,1,0:T(8,128)S(1)}, u32[]{:S(2)}, u32[]{:S(2)}) collective-permute-start(f32[2,1,32,128]{3,2,1,0:T(8,128)S(1)} %get-tuple-element.39), channel_id=1, source_target_pairs={{16,0},{32,16},{48,32},{64,48},{80,64},{96,80},{112,96},{128,112},... | collective-permute-start | bytes 98312 | tf_op jit(solution)/shard_map/ppermute | solution.py:24
  61.1 5.9 %collective-permute-start.12 = (f32[2,18,1,128]{3,2,1,0:T(1,128)S(1)}, f32[2,18,1,128]{3,2,1,0:T(1,128)S(1)}, u32[]{:S(2)}, u32[]{:S(2)}) collective-permute-start(f32[2,18,1,128]{3,2,1,0:T(1,128)S(1)} %get-tuple-element.27), channel_id=1, source_target_pairs={{0,1},{1,2},{2,3},{3,4},{4,5},{5,6},{6,7},{7,8},{8,9},{9,10},{10,1... | collective-permute-start | bytes 55304 | tf_op jit(solution)/shard_map/ppermute | solution.py:21
  63.6 6.6 %collective-permute-start.13 = (f32[2,18,1,128]{3,2,1,0:T(1,128)S(1)}, f32[2,18,1,128]{3,2,1,0:T(1,128)S(1)}, u32[]{:S(2)}, u32[]{:S(2)}) collective-permute-start(f32[2,18,1,128]{3,2,1,0:T(1,128)S(1)} %get-tuple-element.26), channel_id=1, source_target_pairs={{1,0},{2,1},{3,2},{4,3},{5,4},{6,5},{7,6},{8,7},{9,8},{10,9},{11,1... | collective-permute-start | bytes 55304 | tf_op jit(solution)/shard_map/ppermute | solution.py:24
  70.8 5.6 %collective-permute-start.14 = (f32[2,1,32,128]{3,2,1,0:T(8,128)S(1)}, f32[2,1,32,128]{3,2,1,0:T(8,128)S(1)}, u32[]{:S(2)}, u32[]{:S(2)}) collective-permute-start(f32[2,1,32,128]{3,2,1,0:T(8,128)S(1)} %get-tuple-element.36), channel_id=1, source_target_pairs={{0,16},{16,32},{32,48},{48,64},{64,80},{80,96},{96,112},{112,128},... | collective-permute-start | bytes 98312 | tf_op jit(solution)/shard_map/ppermute | solution.py:21
  73.8 6.4 %collective-permute-start.15 = (f32[2,1,32,128]{3,2,1,0:T(8,128)S(1)}, f32[2,1,32,128]{3,2,1,0:T(8,128)S(1)}, u32[]{:S(2)}, u32[]{:S(2)}) collective-permute-start(f32[2,1,32,128]{3,2,1,0:T(8,128)S(1)} %get-tuple-element.37), channel_id=1, source_target_pairs={{16,0},{32,16},{48,32},{64,48},{80,64},{96,80},{112,96},{128,112},... | collective-permute-start | bytes 98312 | tf_op jit(solution)/shard_map/ppermute | solution.py:24
  80.3 5.9 %collective-permute-start.16 = (f32[2,18,1,128]{3,2,1,0:T(1,128)S(1)}, f32[2,18,1,128]{3,2,1,0:T(1,128)S(1)}, u32[]{:S(2)}, u32[]{:S(2)}) collective-permute-start(f32[2,18,1,128]{3,2,1,0:T(1,128)S(1)} %get-tuple-element.25), channel_id=1, source_target_pairs={{0,1},{1,2},{2,3},{3,4},{4,5},{5,6},{6,7},{7,8},{8,9},{9,10},{10,1... | collective-permute-start | bytes 55304 | tf_op jit(solution)/shard_map/ppermute | solution.py:21
  82.8 6.6 %collective-permute-start.17 = (f32[2,18,1,128]{3,2,1,0:T(1,128)S(1)}, f32[2,18,1,128]{3,2,1,0:T(1,128)S(1)}, u32[]{:S(2)}, u32[]{:S(2)}) collective-permute-start(f32[2,18,1,128]{3,2,1,0:T(1,128)S(1)} %get-tuple-element.24), channel_id=1, source_target_pairs={{1,0},{2,1},{3,2},{4,3},{5,4},{6,5},{7,6},{8,7},{9,8},{10,9},{11,1... | collective-permute-start | bytes 55304 | tf_op jit(solution)/shard_map/ppermute | solution.py:24
  90.0 5.6 %collective-permute-start.18 = (f32[2,1,32,128]{3,2,1,0:T(8,128)S(1)}, f32[2,1,32,128]{3,2,1,0:T(8,128)S(1)}, u32[]{:S(2)}, u32[]{:S(2)}) collective-permute-start(f32[2,1,32,128]{3,2,1,0:T(8,128)S(1)} %get-tuple-element.34), channel_id=1, source_target_pairs={{0,16},{16,32},{32,48},{48,64},{64,80},{80,96},{96,112},{112,128},... | collective-permute-start | bytes 98312 | tf_op jit(solution)/shard_map/ppermute | solution.py:21
  93.1 6.4 %collective-permute-start.19 = (f32[2,1,32,128]{3,2,1,0:T(8,128)S(1)}, f32[2,1,32,128]{3,2,1,0:T(8,128)S(1)}, u32[]{:S(2)}, u32[]{:S(2)}) collective-permute-start(f32[2,1,32,128]{3,2,1,0:T(8,128)S(1)} %get-tuple-element.35), channel_id=1, source_target_pairs={{16,0},{32,16},{48,32},{64,48},{80,64},{96,80},{112,96},{128,112},... | collective-permute-start | bytes 98312 | tf_op jit(solution)/shard_map/ppermute | solution.py:24
  99.6 6.1 %collective-permute-start.20 = (f32[2,18,1,128]{3,2,1,0:T(1,128)S(1)}, f32[2,18,1,128]{3,2,1,0:T(1,128)S(1)}, u32[]{:S(2)}, u32[]{:S(2)}) collective-permute-start(f32[2,18,1,128]{3,2,1,0:T(1,128)S(1)} %get-tuple-element.23), channel_id=1, source_target_pairs={{0,1},{1,2},{2,3},{3,4},{4,5},{5,6},{6,7},{7,8},{8,9},{9,10},{10,1... | collective-permute-start | bytes 55304 | tf_op jit(solution)/shard_map/ppermute | solution.py:21
  102.2 6.6 %collective-permute-start.21 = (f32[2,18,1,128]{3,2,1,0:T(1,128)S(1)}, f32[2,18,1,128]{3,2,1,0:T(1,128)S(1)}, u32[]{:S(2)}, u32[]{:S(2)}) collective-permute-start(f32[2,18,1,128]{3,2,1,0:T(1,128)S(1)} %get-tuple-element.22), channel_id=1, source_target_pairs={{1,0},{2,1},{3,2},{4,3},{5,4},{6,5},{7,6},{8,7},{9,8},{10,9},{11,1... | collective-permute-start | bytes 55304 | tf_op jit(solution)/shard_map/ppermute | solution.py:24
  109.4 5.6 %collective-permute-start.22 = (f32[2,1,32,128]{3,2,1,0:T(8,128)S(1)}, f32[2,1,32,128]{3,2,1,0:T(8,128)S(1)}, u32[]{:S(2)}, u32[]{:S(2)}) collective-permute-start(f32[2,1,32,128]{3,2,1,0:T(8,128)S(1)} %get-tuple-element.32), channel_id=1, source_target_pairs={{0,16},{16,32},{32,48},{48,64},{64,80},{80,96},{96,112},{112,128},... | collective-permute-start | bytes 98312 | tf_op jit(solution)/shard_map/ppermute | solution.py:21
  112.4 6.4 %collective-permute-start.23 = (f32[2,1,32,128]{3,2,1,0:T(8,128)S(1)}, f32[2,1,32,128]{3,2,1,0:T(8,128)S(1)}, u32[]{:S(2)}, u32[]{:S(2)}) collective-permute-start(f32[2,1,32,128]{3,2,1,0:T(8,128)S(1)} %get-tuple-element.33), channel_id=1, source_target_pairs={{16,0},{32,16},{48,32},{64,48},{80,64},{96,80},{112,96},{128,112},... | collective-permute-start | bytes 98312 | tf_op jit(solution)/shard_map/ppermute | solution.py:24
  118.9 5.9 %collective-permute-start.24 = (f32[2,18,1,128]{3,2,1,0:T(1,128)S(1)}, f32[2,18,1,128]{3,2,1,0:T(1,128)S(1)}, u32[]{:S(2)}, u32[]{:S(2)}) collective-permute-start(f32[2,18,1,128]{3,2,1,0:T(1,128)S(1)} %get-tuple-element.21), channel_id=1, source_target_pairs={{0,1},{1,2},{2,3},{3,4},{4,5},{5,6},{6,7},{7,8},{8,9},{9,10},{10,1... | collective-permute-start | bytes 55304 | tf_op jit(solution)/shard_map/ppermute | solution.py:21
  121.4 6.6 %collective-permute-start.25 = (f32[2,18,1,128]{3,2,1,0:T(1,128)S(1)}, f32[2,18,1,128]{3,2,1,0:T(1,128)S(1)}, u32[]{:S(2)}, u32[]{:S(2)}) collective-permute-start(f32[2,18,1,128]{3,2,1,0:T(1,128)S(1)} %get-tuple-element.20), channel_id=1, source_target_pairs={{1,0},{2,1},{3,2},{4,3},{5,4},{6,5},{7,6},{8,7},{9,8},{10,9},{11,1... | collective-permute-start | bytes 55304 | tf_op jit(solution)/shard_map/ppermute | solution.py:24
  (5 other events, 29.6 us)
where the time goes:
time: 130 us; the launch traced here: 129 us
  starting transfers between devices  71.9 us (55%)
  waiting for transfers between devices  40.2 us (31%)
  matrix products  9 us (7%)
  other arithmetic  4.93 us (4%)
  local copies, waits for them, and re-layouts  2.65 us (2%)
    ppermute x12, waiting for transfers between devices, with_halo(): lax.ppermute(lax.slice_in_dim(block, 0, width, axis=dim), axis, backward)  40.2 us
    ppermute x12, starting transfers between devices, with_halo(): lax.ppermute(lax.slice_in_dim(block, block.shape[dim] - width, None, axis...  33.2 us
    ppermute x12, starting transfers between devices, with_halo(): lax.ppermute(lax.slice_in_dim(block, 0, width, axis=dim), axis, backward)  30.6 us
    ppermute x2, starting transfers between devices, shifted(): return lax.ppermute(value, axis, pairs)  8.08 us
    dot_general x12, matrix products, apply_data(): trace_rows = jnp.dot(trace_rows, matrix, precision=lax.Precision.HIGHEST)  7.37 us
  transfers between devices with their start and end apart: 26, of which 12 were waited for; matrix products, arithmetic and copies ran while one was open for 9% of the time, Pallas kernels for 0%

commit v1 on v0

v1 whole, which is shorter than its diff:
```python
import jax
import jax.numpy as jnp
from jax import lax
from jax.experimental import pallas as pl
from jax.experimental.pallas import tpu as pltpu
from jax.sharding import PartitionSpec as P

HALF = 20
STEPS = 6
NEAR = 2
F32, BF16 = jnp.float32, jnp.bfloat16
VMEM = pl.BlockSpec(memory_space=pltpu.VMEM)
HBM = pl.BlockSpec(memory_space=pl.ANY)


def pairing(value, axis, offset):
    count = lax.axis_size(axis)
    pairs = []
    for i in range(count):
        other = ((i + offset) ^ 1) - offset
        if 0 <= other < count:
            pairs.append((i, other))
    return lax.ppermute(value, axis, pairs)


def low_part(value):
    return value - value.astype(BF16).astype(F32)


def pieces_x(nv, nc):
    spans, start = {}, 0
    for v in range(nv):
        spans["u", v], start = start, start + STEPS
    for c in range(nc):
        spans["t", c], start = start, start + STEPS
    for v in range(nv):
        spans["low", v], start = start, start + NEAR
    return spans, start


def pieces_z(nv, nc, nx):
    wide = nx + 2 * STEPS
    spans, start = {}, 0
    for d in range(STEPS):
        for v in range(nv):
            spans["u", v, d], start = start, start + wide
        for c in range(nc):
            spans["t", c, d], start = start, start + wide
    for d in range(NEAR):
        for v in range(nv):
            spans["low", v, d], start = start, start + nx
    return spans, start


def padded(rows):
    return -(-rows // 16) * 16


def pack_x(probes, diffusion):
    nv, ni, nx, nt = probes.shape
    nc = diffusion.shape[0]
    spans, each = pieces_x(nv, nc)
    rows = ni * each
    tile = 8

    def kernel(u_hbm, t_hbm, even_ref, odd_ref, u, t, stage, sems):
        copies = []
        for k, first in enumerate((0, nx - tile)):
            copies.append(pltpu.make_async_copy(u_hbm.at[:, :, pl.ds(first, tile), :], u.at[k], sems.at[0, k]))
            copies.append(pltpu.make_async_copy(t_hbm.at[:, :, pl.ds(first, tile), :], t.at[k], sems.at[1, k]))
        for copy in copies:
            copy.start()
        for copy in copies:
            copy.wait()
        for side in range(2):
            first = 0 if side == 0 else tile - STEPS
            near = 0 if side == 0 else tile - NEAR
            for r in range(ni):
                base = r * each
                for v in range(nv):
                    start = base + spans["u", v]
                    stage[side, start : start + STEPS, :] = u[side, v, r, first : first + STEPS, :]
                    start = base + spans["low", v]
                    stage[side, start : start + NEAR, :] = low_part(u[side, v, r, near : near + NEAR, :])
                for c in range(nc):
                    start = base + spans["t", c]
                    stage[side, start : start + STEPS, :] = t[side, c, r, :, :].astype(F32)[first : first + STEPS]
        odd = lax.rem(lax.axis_index("xline"), 2)
        even_ref[...] = stage[1 - odd].astype(BF16)
        odd_ref[...] = stage[odd].astype(BF16)

    out = jax.ShapeDtypeStruct((rows, nt), BF16)
    return pl.pallas_call(
        kernel,
        out_shape=(out, out),
        in_specs=[HBM, HBM],
        out_specs=(VMEM, VMEM),
        scratch_shapes=[
            pltpu.VMEM((2, nv, ni, tile, nt), F32),
            pltpu.VMEM((2, nc, ni, tile, nt), BF16),
            pltpu.VMEM((2, rows, nt), F32),
            pltpu.SemaphoreType.DMA((2, 2)),
        ],
        compiler_params=pltpu.CompilerParams(vmem_limit_bytes=8 << 20),
        name="pack_x",
    )(probes, diffusion)


def gram(wavelet, nt):
    taps = wavelet.shape[0]

    def kernel(w_ref, g_ref, line):
        line[...] = jnp.zeros_like(line)
        line[0:1, 0:taps] = w_ref[...]
        source = lax.broadcasted_iota(jnp.int32, (nt, nt), 0)
        target = lax.broadcasted_iota(jnp.int32, (nt, nt), 1)
        middle = pltpu.roll(line[...], nt - HALF, 1)
        spread = jnp.broadcast_to(middle[0:1, :], (nt, nt))
        band = pltpu.roll(spread, 0, 1, stride=1, stride_axis=0)
        band = jnp.where(jnp.abs(target - source) <= HALF, band, 0.0)
        full = 0.25 * lax.dot_general(band, band, (((1,), (1,)), ((), ())), precision=lax.Precision.HIGHEST)
        high = full.astype(BF16)
        g_ref[0:nt, :] = high
        g_ref[nt : 2 * nt, :] = high
        g_ref[2 * nt : 3 * nt, :] = (full - high.astype(F32)).astype(BF16)

    return pl.pallas_call(
        kernel,
        out_shape=jax.ShapeDtypeStruct((3 * nt, nt), BF16),
        in_specs=[VMEM],
        out_specs=VMEM,
        scratch_shapes=[pltpu.VMEM((8, nt), F32)],
        compiler_params=pltpu.CompilerParams(vmem_limit_bytes=4 << 20),
        cost_estimate=pl.CostEstimate(flops=2 * nt**3, bytes_accessed=4 * nt * nt, transcendentals=0),
        name="gram",
    )(wavelet.reshape(1, taps))


def pack_z(probes, diffusion, even_x, odd_x):
    nv, ni, nx, nt = probes.shape
    nc = diffusion.shape[0]
    x_spans, x_each = pieces_x(nv, nc)
    spans, used = pieces_z(nv, nc, nx)
    rows = padded(used)

    def kernel(u, t, even_x_ref, odd_x_ref, even_ref, odd_ref, halo, stage):
        odd = lax.rem(lax.axis_index("xline"), 2)
        halo[1 - odd] = even_x_ref[...].astype(F32)
        halo[odd] = odd_x_ref[...].astype(F32)
        for side in range(2):
            if rows > used:
                stage[side, used:rows, :] = jnp.zeros((rows - used, nt), F32)
            for d in range(STEPS):
                r = d if side == 0 else ni - STEPS + d
                for kind, count, ref in (("u", nv, u), ("t", nc, t)):
                    for k in range(count):
                        start = spans[kind, k, d]
                        at = r * x_each + x_spans[kind, k]
                        stage[side, start : start + STEPS, :] = halo[0, at : at + STEPS, :]
                        stage[side, start + STEPS : start + STEPS + nx, :] = ref[k, r, :, :].astype(F32)
                        stage[side, start + STEPS + nx : start + 2 * STEPS + nx, :] = halo[1, at : at + STEPS, :]
            for d in range(NEAR):
                r = d if side == 0 else ni - NEAR + d
                for v in range(nv):
                    start = spans["low", v, d]
                    stage[side, start : start + nx, :] = low_part(u[v, r, :, :])
        odd = lax.rem(lax.axis_index("inline"), 2)
        even_ref[...] = stage[1 - odd].astype(BF16)
        odd_ref[...] = stage[odd].astype(BF16)

    out = jax.ShapeDtypeStruct((rows, nt), BF16)
    return pl.pallas_call(
        kernel,
        out_shape=(out, out),
        in_specs=[VMEM] * 4,
        out_specs=(VMEM, VMEM),
        scratch_shapes=[pltpu.VMEM((2, ni * x_each, nt), F32), pltpu.VMEM((2, rows, nt), F32)],
        compiler_params=pltpu.CompilerParams(vmem_limit_bytes=8 << 20),
        name="pack_z",
    )(probes, diffusion, even_x, odd_x)


def sweep(probes, diffusion, even_x, odd_x, even_z, odd_z, matrix):
    nv, ni, nx, nt = probes.shape
    nc = diffusion.shape[0]
    x_spans, x_each = pieces_x(nv, nc)
    z_spans, _ = pieces_z(nv, nc, nx)
    z_rows = even_z.shape[0]
    tile = 8
    height, width = ni + 2 * STEPS, nx + 2 * tile
    left, right = tile - STEPS, tile + nx
    chunk = 7

    def kernel(u0, t0, even_x_ref, odd_x_ref, even_z_ref, odd_z_ref, g_ref, out_hbm, u, t, halo_x, halo_z, data, sems):
        odd = lax.rem(lax.axis_index("xline"), 2)
        halo_x[1 - odd] = even_x_ref[...].astype(F32)
        halo_x[odd] = odd_x_ref[...].astype(F32)
        odd = lax.rem(lax.axis_index("inline"), 2)
        halo_z[1 - odd] = even_z_ref[...].astype(F32)
        halo_z[odd] = odd_z_ref[...].astype(F32)
        inside_in = lax.axis_index("inline") < lax.axis_size("inline") - 1
        inside_x = lax.axis_index("xline") < lax.axis_size("xline") - 1

        for v in range(nv):
            u[v, STEPS : STEPS + ni, tile : tile + nx, :] = u0[v]
        for c in range(nc):
            t[c, STEPS : STEPS + ni, tile : tile + nx, :] = 0.25 * t0[c].astype(F32)
        for r in range(ni):
            e, base = r + STEPS, r * x_each
            for side, first, near in ((0, left, STEPS - NEAR), (1, right, 0)):
                for v in range(nv):
                    at = base + x_spans["u", v]
                    u[v, e, first : first + STEPS, :] = halo_x[side, at : at + STEPS, :]
                    low = base + x_spans["low", v]
                    u[v, e, first + near : first + near + NEAR, :] = (
                        halo_x[side, at + near : at + near + NEAR, :] + halo_x[side, low : low + NEAR, :]
                    )
                for c in range(nc):
                    at = base + x_spans["t", c]
                    t[c, e, first : first + STEPS, :] = 0.25 * halo_x[side, at : at + STEPS, :]
        wide = nx + 2 * STEPS
        for side in range(2):
            for d in range(STEPS):
                e = d if side == 0 else STEPS + ni + d
                for v in range(nv):
                    at = z_spans["u", v, d]
                    u[v, e, left : left + wide, :] = halo_z[side, at : at + wide, :]
                for c in range(nc):
                    at = z_spans["t", c, d]
                    t[c, e, left : left + wide, :] = 0.25 * halo_z[side, at : at + wide, :]
            for d in range(NEAR):
                e = STEPS - NEAR + d if side == 0 else STEPS + ni + d
                for v in range(nv):
                    at = z_spans["low", v, d]
                    u[v, e, tile : tile + nx, :] = u[v, e, tile : tile + nx, :] + halo_z[side, at : at + nx, :]

        g = g_ref[...]
        tensor_of = lambda e: (t[0, e], t[1, e], t[2, e])
        copies = []
        for step in range(1, STEPS + 1):
            first, last = step, height - step
            before = []
            for v in range(nv):
                a, b, _ = tensor_of(first - 1)
                here = u[v, first - 1]
                step_x = pltpu.roll(here, width - 1, 0) - here
                before.append(a * (u[v, first] - here) + b * step_x)
            for low in range(first, last, chunk):
                high = min(low + chunk, last)
                count = high - low
                block = u[:, low:high].reshape(nv * count * width, nt)
                upper = block.astype(BF16)
                lower = (block - upper.astype(F32)).astype(BF16)
                parts = jnp.concatenate([upper, lower, upper], axis=1)
                data[0 : nv * count * width, :] = jnp.dot(parts, g, preferred_element_type=F32)
                for e in range(low, high):
                    a, b, c = tensor_of(e)
                    for v in range(nv):
                        here = u[v, e]
                        step_in = u[v, e + 1] - here
                        step_x = pltpu.roll(here, width - 1, 0) - here
                        flux_in = a * step_in + b * step_x
                        flux_x = b * step_in + c * step_x
                        start = (v * count + e - low) * width
                        turn = (flux_in - before[v]) + (flux_x - pltpu.roll(flux_x, 1, 0))
                        renewed = here - data[start : start + width, :] + turn
                        before[v] = flux_in
                        if e >= STEPS + ni:
                            renewed = jnp.where(inside_in, renewed, 0.0)
                        u[v, e, 0:right, :] = renewed[0:right]
                        u[v, e, right:width, :] = jnp.where(inside_x, renewed[right:width], 0.0)
                if step == STEPS:
                    r = low - STEPS
                    copy = pltpu.make_async_copy(
                        u.at[:, pl.ds(low, count), pl.ds(tile, nx), :],
                        out_hbm.at[:, pl.ds(r, count), :, :],
                        sems.at[len(copies)],
                    )
                    copy.start()
                    copies.append(copy)
        for copy in copies:
            copy.wait()

    return pl.pallas_call(
        kernel,
        out_shape=jax.ShapeDtypeStruct(probes.shape, F32),
        in_specs=[VMEM] * 7,
        out_specs=HBM,
        scratch_shapes=[
            pltpu.VMEM((nv, height, width, nt), F32),
            pltpu.VMEM((nc, height, width, nt), F32),
            pltpu.VMEM((2, ni * x_each, nt), F32),
            pltpu.VMEM((2, z_rows, nt), F32),
            pltpu.VMEM((nv * chunk * width, nt), F32),
            pltpu.SemaphoreType.DMA((8,)),
        ],
        compiler_params=pltpu.CompilerParams(vmem_limit_bytes=24 << 20),
        name="sweep",
    )(probes, diffusion, even_x, odd_x, even_z, odd_z, matrix)


def per_device(probes, diffusion, wavelet):
    even_x, odd_x = pack_x(probes, diffusion)
    even_x, odd_x = pairing(even_x, "xline", 0), pairing(odd_x, "xline", 1)
    matrix = gram(wavelet, probes.shape[-1])
    even_z, odd_z = pack_z(probes, diffusion, even_x, odd_x)
    even_z, odd_z = pairing(even_z, "inline", 0), pairing(odd_z, "inline", 1)
    return sweep(probes, diffusion, even_x, odd_x, even_z, odd_z, matrix)


def solution(mesh):
    return jax.shard_map(
        per_device,
        mesh=mesh,
        in_specs=(P(None, "inline", "xline", None), P(None, "inline", "xline", None), P()),
        out_specs=P(None, "inline", "xline", None),
        check_vma=False,
    )
```

time: 130 us -> 35.3 us (0.27)
  the two profiles are of different devices: /device:TPU:121 before, /device:TPU:9 now
where the time goes in v1:
time: 35.3 us; the launch traced here: 35 us
  starting transfers between devices  16.9 us (48%)
  waiting for transfers between devices  8.95 us (25%)
  Pallas kernels  7.07 us (20%)
  local copies, waits for them, and re-layouts  2.06 us (6%)
    ppermute x4, starting transfers between devices, pairing(): return lax.ppermute(value, axis, pairs)  16.9 us
    ppermute x4, waiting for transfers between devices, pairing(): return lax.ppermute(value, axis, pairs)  8.95 us
    pallas_call x1, Pallas kernels, sweep(): pl.pallas_call(kernel, out_shape=jax.ShapeDtypeStruct(probes.shape, F32),...  6.2 us
    unnamed x10, local copies, waits for them, and re-layouts  2.06 us
  transfers between devices with their start and end apart: 4, of which 2 were waited for; matrix products, arithmetic and copies ran while one was open for 0% of the time, Pallas kernels for 1%

profile of v1, /device:TPU:9, one launch (start us, length us, event | category | flops | bytes accessed | tf_op | source)
XLA Modules:
  0.0 35.0 jit_solution(10844318592111274866)
XLA Ops:
  0.0 0.0 copy-start
  0.0 1.0 %copy-done = f32[2,16,32,128]{3,2,1,0:T(8,128)S(1)} copy-done((f32[2,16,32,128]{3,2,1,0:T(8,128)S(1)}, f32[2,16,32,128]{3,2,1,0:T(8,128)}, u32[]{:S(2)}) %copy-start) | copy-done | bytes 524312
  1.0 0.0 copy-start.2
  1.0 1.0 %copy-done.2 = bf16[3,16,32,128]{3,2,1,0:T(8,128)(2,1)S(1)} copy-done((bf16[3,16,32,128]{3,2,1,0:T(8,128)(2,1)S(1)}, bf16[3,16,32,128]{3,2,1,0:T(8,128)(2,1)}, u32[]{:S(2)}) %copy-start.2) | copy-done | bytes 393240
  2.0 0.2 pack_x.1
  2.3 1.9 %collective-permute-start = (bf16[544,128]{1,0:T(8,128)(2,1)S(1)}, bf16[544,128]{1,0:T(8,128)(2,1)S(1)}, u32[]{:S(2)}, u32[]{:S(2)}) collective-permute-start(bf16[544,128]{1,0:T(8,128)(2,1)S(1)} %get-tuple-element.9), channel_id=1, source_target_pairs={{0,1},{1,0},{2,3},{3,2},{4,5},{5,4},{6,7},{7,6},{8,9},{9,8},{10,11... | collective-permute-start | bytes 417800 | tf_op jit(solution)/shard_map/ppermute | solution.py:23
  4.2 0.0 copy-start.1
  4.2 0.0 copy-start.3
  4.2 4.3 %collective-permute-start.1 = (bf16[544,128]{1,0:T(8,128)(2,1)S(1)}, bf16[544,128]{1,0:T(8,128)(2,1)S(1)}, u32[]{:S(2)}, u32[]{:S(2)}) collective-permute-start(bf16[544,128]{1,0:T(8,128)(2,1)S(1)} %get-tuple-element.10), channel_id=1, source_target_pairs={{1,2},{2,1},{3,4},{4,3},{5,6},{6,5},{7,8},{8,7},{9,10},{10,9},{11,... | collective-permute-start | bytes 417800 | tf_op jit(solution)/shard_map/ppermute | solution.py:23
  8.6 0.0 collective-permute-done.even_x_ref
  8.6 2.4 %collective-permute-done.1.odd_x_ref = bf16[544,128]{1,0:T(8,128)(2,1)S(1)} collective-permute-done((bf16[544,128]{1,0:T(8,128)(2,1)S(1)}, bf16[544,128]{1,0:T(8,128)(2,1)S(1)}, u32[]{:S(2)}, u32[]{:S(2)}) %collective-permute-start.1) | collective-permute-done | bytes 139296 | tf_op jit(solution)/shard_map/ppermute | solution.py:23
  11.0 0.2 pack_z.1
  11.2 8.7 %collective-permute-start.2 = (bf16[1456,128]{1,0:T(8,128)(2,1)S(1)}, bf16[1456,128]{1,0:T(8,128)(2,1)S(1)}, u32[]{:S(2)}, u32[]{:S(2)}) collective-permute-start(bf16[1456,128]{1,0:T(8,128)(2,1)S(1)} %get-tuple-element.11), channel_id=1, source_target_pairs={{0,16},{16,0},{32,48},{48,32},{64,80},{80,64},{96,112},{112,96},{1... | collective-permute-start | bytes 1118216 | tf_op jit(solution)/shard_map/ppermute | solution.py:23
  19.9 0.0 copy-start.4
  19.9 1.9 %collective-permute-start.3 = (bf16[1456,128]{1,0:T(8,128)(2,1)S(1)}, bf16[1456,128]{1,0:T(8,128)(2,1)S(1)}, u32[]{:S(2)}, u32[]{:S(2)}) collective-permute-start(bf16[1456,128]{1,0:T(8,128)(2,1)S(1)} %get-tuple-element.12), channel_id=1, source_target_pairs={{16,32},{32,16},{48,64},{64,48},{80,96},{96,80},{112,128},{128,112... | collective-permute-start | bytes 1118216 | tf_op jit(solution)/shard_map/ppermute | solution.py:23
  21.9 0.0 copy-done.4
  21.9 0.4 %gram.1.g_ref = bf16[384,128]{1,0:T(8,128)(2,1)S(1)} custom-call(f32[1,41]{1,0:T(1,128)S(1)} %bitcast.1), custom_call_target="tpu_custom_call" | custom-call | flops 4194304 | bytes 65536 | tf_op jit(solution)/shard_map/gram/pallas_call | solution.py:127
  22.3 0.0 collective-permute-done.2.even_z_ref
  22.3 6.5 %collective-permute-done.3.odd_z_ref = bf16[1456,128]{1,0:T(8,128)(2,1)S(1)} collective-permute-done((bf16[1456,128]{1,0:T(8,128)(2,1)S(1)}, bf16[1456,128]{1,0:T(8,128)(2,1)S(1)}, u32[]{:S(2)}, u32[]{:S(2)}) %collective-permute-start.3) | collective-permute-done | bytes 372768 | tf_op jit(solution)/shard_map/ppermute | solution.py:23
  28.8 0.0 copy-done.1
  28.8 0.0 copy-done.3
  28.8 6.2 %sweep.1 = f32[2,16,32,128]{3,2,1,0:T(8,128)} custom-call(f32[2,16,32,128]{3,2,1,0:T(8,128)S(1)} %copy-done.1, bf16[3,16,32,128]{3,2,1,0:T(8,128)(2,1)S(1)} %copy-done.3, bf16[544,128]{1,0:T(8,128)(2,1)S(1)} %collective-permute-done.even_x_ref, bf16[544,128]{1,0:T(8,128)(2,1)S(1)} %collective-permute-done.1.odd_x_ref, ...), custom_call_target="tpu_custom_call" | custom-call | tf_op jit(solution)/shard_map/sweep/pallas_call | solution.py:284
Async XLA Ops:
  0.0 1.0 %copy-start = (f32[2,16,32,128]{3,2,1,0:T(8,128)S(1)}, f32[2,16,32,128]{3,2,1,0:T(8,128)}, u32[]{:S(2)}) copy-start(f32[2,16,32,128]{3,2,1,0:T(8,128)} %u0.1) | copy-start | bytes 1572868
  1.0 1.0 %copy-start.2 = (bf16[3,16,32,128]{3,2,1,0:T(8,128)(2,1)S(1)}, bf16[3,16,32,128]{3,2,1,0:T(8,128)(2,1)}, u32[]{:S(2)}) copy-start(bf16[3,16,32,128]{3,2,1,0:T(8,128)(2,1)} %t0.1) | copy-start | bytes 1179652
  2.3 6.3 %collective-permute-start = (bf16[544,128]{1,0:T(8,128)(2,1)S(1)}, bf16[544,128]{1,0:T(8,128)(2,1)S(1)}, u32[]{:S(2)}, u32[]{:S(2)}) collective-permute-start(bf16[544,128]{1,0:T(8,128)(2,1)S(1)} %get-tuple-element.9), channel_id=1, source_target_pairs={{0,1},{1,0},{2,3},{3,2},{4,5},{5,4},{6,7},{7,6},{8,9},{9,8},{10,11... | collective-permute-start | bytes 417800 | tf_op jit(solution)/shard_map/ppermute | solution.py:23
  4.2 24.6 %copy-start.1 = (f32[2,16,32,128]{3,2,1,0:T(8,128)S(1)}, f32[2,16,32,128]{3,2,1,0:T(8,128)}, u32[]{:S(2)}) copy-start(f32[2,16,32,128]{3,2,1,0:T(8,128)} %u0.1) | copy-start | bytes 1572868
  4.2 24.6 %copy-start.3 = (bf16[3,16,32,128]{3,2,1,0:T(8,128)(2,1)S(1)}, bf16[3,16,32,128]{3,2,1,0:T(8,128)(2,1)}, u32[]{:S(2)}) copy-start(bf16[3,16,32,128]{3,2,1,0:T(8,128)(2,1)} %t0.1) | copy-start | bytes 1179652
  4.2 6.8 %collective-permute-start.1 = (bf16[544,128]{1,0:T(8,128)(2,1)S(1)}, bf16[544,128]{1,0:T(8,128)(2,1)S(1)}, u32[]{:S(2)}, u32[]{:S(2)}) collective-permute-start(bf16[544,128]{1,0:T(8,128)(2,1)S(1)} %get-tuple-element.10), channel_id=1, source_target_pairs={{1,2},{2,1},{3,4},{4,3},{5,6},{6,5},{7,8},{8,7},{9,10},{10,9},{11,... | collective-permute-start | bytes 417800 | tf_op jit(solution)/shard_map/ppermute | solution.py:23
  11.2 11.1 %collective-permute-start.2 = (bf16[1456,128]{1,0:T(8,128)(2,1)S(1)}, bf16[1456,128]{1,0:T(8,128)(2,1)S(1)}, u32[]{:S(2)}, u32[]{:S(2)}) collective-permute-start(bf16[1456,128]{1,0:T(8,128)(2,1)S(1)} %get-tuple-element.11), channel_id=1, source_target_pairs={{0,16},{16,0},{32,48},{48,32},{64,80},{80,64},{96,112},{112,96},{1... | collective-permute-start | bytes 1118216 | tf_op jit(solution)/shard_map/ppermute | solution.py:23
  19.9 1.9 %copy-start.4 = (f32[41]{0:T(128)S(1)}, f32[41]{0:T(128)}, u32[]{:S(2)}) copy-start(f32[41]{0:T(128)} %param.5) | copy-start | bytes 496
  19.9 8.9 %collective-permute-start.3 = (bf16[1456,128]{1,0:T(8,128)(2,1)S(1)}, bf16[1456,128]{1,0:T(8,128)(2,1)S(1)}, u32[]{:S(2)}, u32[]{:S(2)}) collective-permute-start(bf16[1456,128]{1,0:T(8,128)(2,1)S(1)} %get-tuple-element.12), channel_id=1, source_target_pairs={{16,32},{32,16},{48,64},{64,48},{80,96},{96,80},{112,128},{128,112... | collective-permute-start | bytes 1118216 | tf_op jit(solution)/shard_map/ppermute | solution.py:23

commit v2 on v1

--- a/solution.py
+++ b/solution.py
@@ -10,7 +10,7 @@
 NEAR = 2
 F32, BF16 = jnp.float32, jnp.bfloat16
 VMEM = pl.BlockSpec(memory_space=pltpu.VMEM)
-HBM = pl.BlockSpec(memory_space=pl.ANY)
+HBM = pl.BlockSpec(memory_space=pltpu.HBM)
 
 
 def pairing(value, axis, offset):
@@ -56,20 +56,44 @@
     return -(-rows // 16) * 16
 
 
+def parity(axis):
+    return lax.rem(lax.axis_index(axis), 2)
+
+
+def pieces_o(nv, nc):
+    names = [("u", v, d) for d in range(STEPS) for v in range(nv)]
+    names += [("low", v, d) for d in range(NEAR) for v in range(nv)]
+    names += [("t", c, d) for c in range(nc) for d in range(STEPS)]
+    return {name: k for k, name in enumerate(names)}
+
+
 def pack_x(probes, diffusion):
     nv, ni, nx, nt = probes.shape
     nc = diffusion.shape[0]
     spans, each = pieces_x(nv, nc)
-    rows = ni * each
+    o_pieces = pieces_o(nv, nc)
+    rows, o_rows = ni * each, len(o_pieces) * nx
     tile = 8
 
-    def kernel(u_hbm, t_hbm, even_ref, odd_ref, u, t, stage, sems):
+    def kernel(u_hbm, t_hbm, even_ref, odd_ref, o_ref, u, t, u_o, stage, sems):
+        odd_in = parity("inline")
+        edge = odd_in * (ni - STEPS)
         copies = []
         for k, first in enumerate((0, nx - tile)):
             copies.append(pltpu.make_async_copy(u_hbm.at[:, :, pl.ds(first, tile), :], u.at[k], sems.at[0, k]))
             copies.append(pltpu.make_async_copy(t_hbm.at[:, :, pl.ds(first, tile), :], t.at[k], sems.at[1, k]))
+        copies.append(pltpu.make_async_copy(u_hbm.at[:, pl.ds(edge, STEPS)], u_o, sems.at[2, 0]))
         for copy in copies:
             copy.start()
+        direct = []
+        for c in range(nc):
+            at = o_pieces["t", c, 0] * nx
+            for d in range(STEPS):
+                copy = pltpu.make_async_copy(
+                    t_hbm.at[c, edge + d], o_ref.at[pl.ds(at + d * nx, nx), :], sems.at[3 + c, d]
+                )
+                copy.start()
+                direct.append(copy)
         for copy in copies:
             copy.wait()
         for side in range(2):
@@ -85,23 +109,33 @@
                 for c in range(nc):
                     start = base + spans["t", c]
                     stage[side, start : start + STEPS, :] = t[side, c, r, :, :].astype(F32)[first : first + STEPS]
-        odd = lax.rem(lax.axis_index("xline"), 2)
+        odd = parity("xline")
         even_ref[...] = stage[1 - odd].astype(BF16)
         odd_ref[...] = stage[odd].astype(BF16)
+        near = odd_in * (STEPS - NEAR)
+        for v in range(nv):
+            for d in range(STEPS):
+                at = o_pieces["u", v, d] * nx
+                o_ref[at : at + nx, :] = u_o[v, d].astype(BF16)
+            for d in range(NEAR):
+                at = o_pieces["low", v, d] * nx
+                o_ref[at : at + nx, :] = low_part(u_o[v, near + d]).astype(BF16)
+        for copy in direct:
+            copy.wait()
 
     out = jax.ShapeDtypeStruct((rows, nt), BF16)
     return pl.pallas_call(
         kernel,
-        out_shape=(out, out),
+        out_shape=(out, out, jax.ShapeDtypeStruct((o_rows, nt), BF16)),
         in_specs=[HBM, HBM],
-        out_specs=(VMEM, VMEM),
+        out_specs=(VMEM, VMEM, VMEM),
         scratch_shapes=[
             pltpu.VMEM((2, nv, ni, tile, nt), F32),
             pltpu.VMEM((2, nc, ni, tile, nt), BF16),
+            pltpu.VMEM((nv, STEPS, nx, nt), F32),
             pltpu.VMEM((2, rows, nt), F32),
-            pltpu.SemaphoreType.DMA((2, 2)),
+            pltpu.SemaphoreType.DMA((3 + nc, STEPS)),
         ],
-        compiler_params=pltpu.CompilerParams(vmem_limit_bytes=8 << 20),
         name="pack_x",
     )(probes, diffusion)
 
@@ -141,63 +175,78 @@
     nc = diffusion.shape[0]
     x_spans, x_each = pieces_x(nv, nc)
     spans, used = pieces_z(nv, nc, nx)
-    rows = padded(used)
-
-    def kernel(u, t, even_x_ref, odd_x_ref, even_ref, odd_ref, halo, stage):
-        odd = lax.rem(lax.axis_index("xline"), 2)
+    corners, c_used = pieces_z(nv, nc, 0)
+    rows, c_rows = padded(used), padded(c_used)
+
+    def kernel(u, t, even_x_ref, odd_x_ref, e_ref, c_ref, halo, stage, stage_c):
+        odd = parity("xline")
         halo[1 - odd] = even_x_ref[...].astype(F32)
         halo[odd] = odd_x_ref[...].astype(F32)
         for side in range(2):
             if rows > used:
                 stage[side, used:rows, :] = jnp.zeros((rows - used, nt), F32)
+            if c_rows > c_used:
+                stage_c[side, c_used:c_rows, :] = jnp.zeros((c_rows - c_used, nt), F32)
             for d in range(STEPS):
                 r = d if side == 0 else ni - STEPS + d
                 for kind, count, ref in (("u", nv, u), ("t", nc, t)):
                     for k in range(count):
                         start = spans[kind, k, d]
                         at = r * x_each + x_spans[kind, k]
-                        stage[side, start : start + STEPS, :] = halo[0, at : at + STEPS, :]
+                        on_left, on_right = halo[0, at : at + STEPS, :], halo[1, at : at + STEPS, :]
+                        stage[side, start : start + STEPS, :] = on_left
                         stage[side, start + STEPS : start + STEPS + nx, :] = ref[k, r, :, :].astype(F32)
-                        stage[side, start + STEPS + nx : start + 2 * STEPS + nx, :] = halo[1, at : at + STEPS, :]
+                        stage[side, start + STEPS + nx : start + 2 * STEPS + nx, :] = on_right
+                        start = corners[kind, k, d]
+                        stage_c[side, start : start + STEPS, :] = on_left
+                        stage_c[side, start + STEPS : start + 2 * STEPS, :] = on_right
             for d in range(NEAR):
                 r = d if side == 0 else ni - NEAR + d
                 for v in range(nv):
                     start = spans["low", v, d]
                     stage[side, start : start + nx, :] = low_part(u[v, r, :, :])
-        odd = lax.rem(lax.axis_index("inline"), 2)
-        even_ref[...] = stage[1 - odd].astype(BF16)
-        odd_ref[...] = stage[odd].astype(BF16)
-
-    out = jax.ShapeDtypeStruct((rows, nt), BF16)
+        odd = parity("inline")
+        c_ref[...] = stage_c[odd].astype(BF16)
+        e_ref[...] = stage[1 - odd].astype(BF16)
+
     return pl.pallas_call(
         kernel,
-        out_shape=(out, out),
+        out_shape=(jax.ShapeDtypeStruct((rows, nt), BF16), jax.ShapeDtypeStruct((c_rows, nt), BF16)),
         in_specs=[VMEM] * 4,
         out_specs=(VMEM, VMEM),
-        scratch_shapes=[pltpu.VMEM((2, ni * x_each, nt), F32), pltpu.VMEM((2, rows, nt), F32)],
+        scratch_shapes=[
+            pltpu.VMEM((2, ni * x_each, nt), F32),
+            pltpu.VMEM((2, rows, nt), F32),
+            pltpu.VMEM((2, c_rows, nt), F32),
+        ],
         compiler_params=pltpu.CompilerParams(vmem_limit_bytes=8 << 20),
         name="pack_z",
     )(probes, diffusion, even_x, odd_x)
 
 
-def sweep(probes, diffusion, even_x, odd_x, even_z, odd_z, matrix):
+def sweep(probes, diffusion, even_x, odd_x, e_rows, o_rows, c_rows, matrix):
     nv, ni, nx, nt = probes.shape
     nc = diffusion.shape[0]
     x_spans, x_each = pieces_x(nv, nc)
     z_spans, _ = pieces_z(nv, nc, nx)
-    z_rows = even_z.shape[0]
+    corners, _ = pieces_z(nv, nc, 0)
+    o_pieces = pieces_o(nv, nc)
     tile = 8
     height, width = ni + 2 * STEPS, nx + 2 * tile
     left, right = tile - STEPS, tile + nx
     chunk = 7
 
-    def kernel(u0, t0, even_x_ref, odd_x_ref, even_z_ref, odd_z_ref, g_ref, out_hbm, u, t, halo_x, halo_z, data, sems):
-        odd = lax.rem(lax.axis_index("xline"), 2)
+    def kernel(u0, t0, even_x_ref, odd_x_ref, e_ref, o_ref, c_ref, g_ref, out_hbm, u, t, halo_x, halo_e, halo_c, data, sems):
+        odd = parity("xline")
         halo_x[1 - odd] = even_x_ref[...].astype(F32)
         halo_x[odd] = odd_x_ref[...].astype(F32)
-        odd = lax.rem(lax.axis_index("inline"), 2)
-        halo_z[1 - odd] = even_z_ref[...].astype(F32)
-        halo_z[odd] = odd_z_ref[...].astype(F32)
+        halo_e[...] = e_ref[...].astype(F32)
+        halo_c[...] = c_ref[...].astype(F32)
+        odd_in = parity("inline")
+        far = STEPS + ni
+        e_first, o_first = (1 - odd_in) * far, odd_in * far
+        e_near = e_first + odd_in * (STEPS - NEAR)
+        o_near = o_first + (1 - odd_in) * (STEPS - NEAR)
         inside_in = lax.axis_index("inline") < lax.axis_size("inline") - 1
         inside_x = lax.axis_index("xline") < lax.axis_size("xline") - 1
 
@@ -219,20 +268,24 @@
                     at = base + x_spans["t", c]
                     t[c, e, first : first + STEPS, :] = 0.25 * halo_x[side, at : at + STEPS, :]
         wide = nx + 2 * STEPS
-        for side in range(2):
-            for d in range(STEPS):
-                e = d if side == 0 else STEPS + ni + d
-                for v in range(nv):
-                    at = z_spans["u", v, d]
-                    u[v, e, left : left + wide, :] = halo_z[side, at : at + wide, :]
-                for c in range(nc):
-                    at = z_spans["t", c, d]
-                    t[c, e, left : left + wide, :] = 0.25 * halo_z[side, at : at + wide, :]
-            for d in range(NEAR):
-                e = STEPS - NEAR + d if side == 0 else STEPS + ni + d
-                for v in range(nv):
-                    at = z_spans["low", v, d]
-                    u[v, e, tile : tile + nx, :] = u[v, e, tile : tile + nx, :] + halo_z[side, at : at + nx, :]
+        for d in range(STEPS):
+            e, o = e_first + d, o_first + d
+            for kind, count, ref, scale in (("u", nv, u, 1.0), ("t", nc, t, 0.25)):
+                for k in range(count):
+                    at = z_spans[kind, k, d]
+                    ref[k, e, left : left + wide, :] = scale * halo_e[at : at + wide, :]
+                    at = corners[kind, k, d]
+                    ref[k, o, left : left + STEPS, :] = scale * halo_c[at : at + STEPS, :]
+                    ref[k, o, right : right + STEPS, :] = scale * halo_c[at + STEPS : at + 2 * STEPS, :]
+                    at = o_pieces[kind, k, d] * nx
+                    ref[k, o, tile : tile + nx, :] = scale * o_ref[at : at + nx, :].astype(F32)
+        for d in range(NEAR):
+            e, o = e_near + d, o_near + d
+            for v in range(nv):
+                at = z_spans["low", v, d]
+                u[v, e, tile : tile + nx, :] = u[v, e, tile : tile + nx, :] + halo_e[at : at + nx, :]
+                at = o_pieces["low", v, d] * nx
+                u[v, o, tile : tile + nx, :] = u[v, o, tile : tile + nx, :] + o_ref[at : at + nx, :].astype(F32)
 
         g = g_ref[...]
         tensor_of = lambda e: (t[0, e], t[1, e], t[2, e])
@@ -284,28 +337,32 @@
     return pl.pallas_call(
         kernel,
         out_shape=jax.ShapeDtypeStruct(probes.shape, F32),
-        in_specs=[VMEM] * 7,
+        in_specs=[VMEM] * 8,
         out_specs=HBM,
         scratch_shapes=[
             pltpu.VMEM((nv, height, width, nt), F32),
             pltpu.VMEM((nc, height, width, nt), F32),
             pltpu.VMEM((2, ni * x_each, nt), F32),
-            pltpu.VMEM((2, z_rows, nt), F32),
+            pltpu.VMEM((e_rows.shape[0], nt), F32),
+            pltpu.VMEM((c_rows.shape[0], nt), F32),
             pltpu.VMEM((nv * chunk * width, nt), F32),
             pltpu.SemaphoreType.DMA((8,)),
         ],
         compiler_params=pltpu.CompilerParams(vmem_limit_bytes=24 << 20),
         name="sweep",
-    )(probes, diffusion, even_x, odd_x, even_z, odd_z, matrix)
+    )(probes, diffusion, even_x, odd_x, e_rows, o_rows, c_rows, matrix)
 
 
 def per_device(probes, diffusion, wavelet):
-    even_x, odd_x = pack_x(probes, diffusion)
-    even_x, odd_x = pairing(even_x, "xline", 0), pairing(odd_x, "xline", 1)
+    even_x, odd_x, o_rows = pack_x(probes, diffusion)
+    odd_x = pairing(odd_x, "xline", 1)
+    even_x = pairing(even_x, "xline", 0)
+    o_rows = pairing(o_rows, "inline", 1)
     matrix = gram(wavelet, probes.shape[-1])
-    even_z, odd_z = pack_z(probes, diffusion, even_x, odd_x)
-    even_z, odd_z = pairing(even_z, "inline", 0), pairing(odd_z, "inline", 1)
-    return sweep(probes, diffusion, even_x, odd_x, even_z, odd_z, matrix)
+    e_rows, c_rows = pack_z(probes, diffusion, even_x, odd_x)
+    c_rows = pairing(c_rows, "inline", 1)
+    e_rows = pairing(e_rows, "inline", 0)
+    return sweep(probes, diffusion, even_x, odd_x, e_rows, o_rows, c_rows, matrix)
 
 
 def solution(mesh):

time: 35.3 us -> 36.4 us (1.031)
  the two profiles are of different devices: /device:TPU:9 before, /device:TPU:227 now
where the time goes in v2:
time: 36.4 us; the launch traced here: 36.2 us
  starting transfers between devices  17.6 us (48%)
  waiting for transfers between devices  9.25 us (25%)
  Pallas kernels  9.2 us (25%)
    ppermute x5, starting transfers between devices, pairing(): return lax.ppermute(value, axis, pairs)  17.6 us
    ppermute x5, waiting for transfers between devices, pairing(): return lax.ppermute(value, axis, pairs)  9.25 us
    pallas_call x1, Pallas kernels, sweep(): pl.pallas_call(kernel, out_shape=jax.ShapeDtypeStruct(probes.shape, F32),...  6.05 us
    pallas_call x1, Pallas kernels, pack_x(): pl.pallas_call(kernel, out_shape=(out, out, jax.ShapeDtypeStruct((o_rows,...  2.51 us
  transfers between devices with their start and end apart: 5, of which 2 were waited for; matrix products, arithmetic and copies ran while one was open for 0% of the time, Pallas kernels for 1%

profile of v2, /device:TPU:227, one launch (start us, length us, event | category | flops | bytes accessed | tf_op | source)
XLA Modules:
  0.0 36.2 jit_solution(8319706213901071659)
XLA Ops:
  0.0 0.0 copy-start.1
  0.0 0.0 copy-start
  0.0 2.5 %pack_x.1 = (bf16[544,128]{1,0:T(8,128)(2,1)}, bf16[544,128]{1,0:T(8,128)(2,1)}, bf16[1088,128]{1,0:T(8,128)(2,1)}) custom-call(f32[2,16,32,128]{3,2,1,0:T(8,128)} %u0.1, bf16[3,16,32,128]{3,2,1,0:T(8,128)(2,1)} %t0.1), custom_call_target="tpu_custom_call" | custom-call | tf_op jit(solution)/shard_map/pack_x/pallas_call | solution.py:127
  2.5 3.2 %collective-permute-start = (bf16[544,128]{1,0:T(8,128)(2,1)}, bf16[544,128]{1,0:T(8,128)(2,1)S(1)}, u32[]{:S(2)}, u32[]{:S(2)}) collective-permute-start(bf16[544,128]{1,0:T(8,128)(2,1)} %get-tuple-element.10), channel_id=1, source_target_pairs={{0,1},{1,0},{2,3},{3,2},{4,5},{5,4},{6,7},{7,6},{8,9},{9,8},{10,11... | collective-permute-start | bytes 417800 | tf_op jit(solution)/shard_map/ppermute | solution.py:23
  5.7 0.0 copy-start.3
  5.8 3.9 %collective-permute-start.1 = (bf16[544,128]{1,0:T(8,128)(2,1)}, bf16[544,128]{1,0:T(8,128)(2,1)S(1)}, u32[]{:S(2)}, u32[]{:S(2)}) collective-permute-start(bf16[544,128]{1,0:T(8,128)(2,1)} %get-tuple-element.11), channel_id=1, source_target_pairs={{1,2},{2,1},{3,4},{4,3},{5,6},{6,5},{7,8},{8,7},{9,10},{10,9},{11,... | collective-permute-start | bytes 417800 | tf_op jit(solution)/shard_map/ppermute | solution.py:23
  9.7 0.0 collective-permute-done.even_x_ref
  9.7 4.7 %collective-permute-done.1.odd_x_ref = bf16[544,128]{1,0:T(8,128)(2,1)S(1)} collective-permute-done((bf16[544,128]{1,0:T(8,128)(2,1)}, bf16[544,128]{1,0:T(8,128)(2,1)S(1)}, u32[]{:S(2)}, u32[]{:S(2)}) %collective-permute-start.1) | collective-permute-done | bytes 139296 | tf_op jit(solution)/shard_map/ppermute | solution.py:23
  14.4 0.0 copy-done.1
  14.4 0.0 copy-done
  14.4 0.2 pack_z.1
  14.6 3.7 %collective-permute-start.2 = (bf16[1456,128]{1,0:T(8,128)(2,1)S(1)}, bf16[1456,128]{1,0:T(8,128)(2,1)S(1)}, u32[]{:S(2)}, u32[]{:S(2)}) collective-permute-start(bf16[1456,128]{1,0:T(8,128)(2,1)S(1)} %get-tuple-element.12), channel_id=1, source_target_pairs={{0,16},{16,0},{32,48},{48,32},{64,80},{80,64},{96,112},{112,96},{1... | collective-permute-start | bytes 1118216 | tf_op jit(solution)/shard_map/ppermute | solution.py:23
  18.3 0.0 copy-done.3
  18.4 4.7 %collective-permute-start.3 = (bf16[1088,128]{1,0:T(8,128)(2,1)S(1)}, bf16[1088,128]{1,0:T(8,128)(2,1)S(1)}, u32[]{:S(2)}, u32[]{:S(2)}) collective-permute-start(bf16[1088,128]{1,0:T(8,128)(2,1)S(1)} %copy-done.3), channel_id=1, source_target_pairs={{16,32},{32,16},{48,64},{64,48},{80,96},{96,80},{112,128},{128,112... | collective-permute-start | bytes 835592 | tf_op jit(solution)/shard_map/ppermute | solution.py:23
  23.0 0.0 copy-start.2
  23.0 2.1 %collective-permute-start.4 = (bf16[368,128]{1,0:T(8,128)(2,1)S(1)}, bf16[368,128]{1,0:T(8,128)(2,1)S(1)}, u32[]{:S(2)}, u32[]{:S(2)}) collective-permute-start(bf16[368,128]{1,0:T(8,128)(2,1)S(1)} %get-tuple-element.14), channel_id=1, source_target_pairs={{16,32},{32,16},{48,64},{64,48},{80,96},{96,80},{112,128},{128,112... | collective-permute-start | bytes 282632 | tf_op jit(solution)/shard_map/ppermute | solution.py:23
  25.2 0.0 copy-done.2
  25.2 0.4 %gram.1.g_ref = bf16[384,128]{1,0:T(8,128)(2,1)S(1)} custom-call(f32[1,41]{1,0:T(1,128)S(1)} %bitcast.1), custom_call_target="tpu_custom_call" | custom-call | flops 4194304 | bytes 65536 | tf_op jit(solution)/shard_map/gram/pallas_call | solution.py:161
  25.6 4.6 %collective-permute-done.4.c_ref = bf16[368,128]{1,0:T(8,128)(2,1)S(1)} collective-permute-done((bf16[368,128]{1,0:T(8,128)(2,1)S(1)}, bf16[368,128]{1,0:T(8,128)(2,1)S(1)}, u32[]{:S(2)}, u32[]{:S(2)}) %collective-permute-start.4) | collective-permute-done | bytes 94240 | tf_op jit(solution)/shard_map/ppermute | solution.py:23
  30.1 0.0 collective-permute-done.3.o_ref
  30.1 0.0 collective-permute-done.2.e_ref
  30.1 6.0 %sweep.1 = f32[2,16,32,128]{3,2,1,0:T(8,128)} custom-call(f32[2,16,32,128]{3,2,1,0:T(8,128)S(1)} %copy-done, bf16[3,16,32,128]{3,2,1,0:T(8,128)(2,1)S(1)} %copy-done.1, bf16[544,128]{1,0:T(8,128)(2,1)S(1)} %collective-permute-done.even_x_ref, bf16[544,128]{1,0:T(8,128)(2,1)S(1)} %collective-permute-done.1.odd_x_ref, ...), custom_call_target="tpu_custom_call" | custom-call | tf_op jit(solution)/shard_map/sweep/pallas_call | solution.py:337
Async XLA Ops:
  0.0 14.4 %copy-start.1 = (bf16[3,16,32,128]{3,2,1,0:T(8,128)(2,1)S(1)}, bf16[3,16,32,128]{3,2,1,0:T(8,128)(2,1)}, u32[]{:S(2)}) copy-start(bf16[3,16,32,128]{3,2,1,0:T(8,128)(2,1)} %t0.1) | copy-start | bytes 1179652
  0.0 14.4 %copy-start = (f32[2,16,32,128]{3,2,1,0:T(8,128)S(1)}, f32[2,16,32,128]{3,2,1,0:T(8,128)}, u32[]{:S(2)}) copy-start(f32[2,16,32,128]{3,2,1,0:T(8,128)} %u0.1) | copy-start | bytes 1572868
  2.5 7.1 %collective-permute-start = (bf16[544,128]{1,0:T(8,128)(2,1)}, bf16[544,128]{1,0:T(8,128)(2,1)S(1)}, u32[]{:S(2)}, u32[]{:S(2)}) collective-permute-start(bf16[544,128]{1,0:T(8,128)(2,1)} %get-tuple-element.10), channel_id=1, source_target_pairs={{0,1},{1,0},{2,3},{3,2},{4,5},{5,4},{6,7},{7,6},{8,9},{9,8},{10,11... | collective-permute-start | bytes 417800 | tf_op jit(solution)/shard_map/ppermute | solution.py:23
  5.7 12.6 %copy-start.3 = (bf16[1088,128]{1,0:T(8,128)(2,1)S(1)}, bf16[1088,128]{1,0:T(8,128)(2,1)}, u32[]{:S(2)}) copy-start(bf16[1088,128]{1,0:T(8,128)(2,1)} %get-tuple-element.13) | copy-start | bytes 835588
  5.8 8.6 %collective-permute-start.1 = (bf16[544,128]{1,0:T(8,128)(2,1)}, bf16[544,128]{1,0:T(8,128)(2,1)S(1)}, u32[]{:S(2)}, u32[]{:S(2)}) collective-permute-start(bf16[544,128]{1,0:T(8,128)(2,1)} %get-tuple-element.11), channel_id=1, source_target_pairs={{1,2},{2,1},{3,4},{4,3},{5,6},{6,5},{7,8},{8,7},{9,10},{10,9},{11,... | collective-permute-start | bytes 417800 | tf_op jit(solution)/shard_map/ppermute | solution.py:23
  14.6 15.5 %collective-permute-start.2 = (bf16[1456,128]{1,0:T(8,128)(2,1)S(1)}, bf16[1456,128]{1,0:T(8,128)(2,1)S(1)}, u32[]{:S(2)}, u32[]{:S(2)}) collective-permute-start(bf16[1456,128]{1,0:T(8,128)(2,1)S(1)} %get-tuple-element.12), channel_id=1, source_target_pairs={{0,16},{16,0},{32,48},{48,32},{64,80},{80,64},{96,112},{112,96},{1... | collective-permute-start | bytes 1118216 | tf_op jit(solution)/shard_map/ppermute | solution.py:23
  18.4 11.8 %collective-permute-start.3 = (bf16[1088,128]{1,0:T(8,128)(2,1)S(1)}, bf16[1088,128]{1,0:T(8,128)(2,1)S(1)}, u32[]{:S(2)}, u32[]{:S(2)}) collective-permute-start(bf16[1088,128]{1,0:T(8,128)(2,1)S(1)} %copy-done.3), channel_id=1, source_target_pairs={{16,32},{32,16},{48,64},{64,48},{80,96},{96,80},{112,128},{128,112... | collective-permute-start | bytes 835592 | tf_op jit(solution)/shard_map/ppermute | solution.py:23
  23.0 2.1 %copy-start.2 = (f32[41]{0:T(128)S(1)}, f32[41]{0:T(128)}, u32[]{:S(2)}) copy-start(f32[41]{0:T(128)} %param.5) | copy-start | bytes 496
  23.0 7.1 %collective-permute-start.4 = (bf16[368,128]{1,0:T(8,128)(2,1)S(1)}, bf16[368,128]{1,0:T(8,128)(2,1)S(1)}, u32[]{:S(2)}, u32[]{:S(2)}) collective-permute-start(bf16[368,128]{1,0:T(8,128)(2,1)S(1)} %get-tuple-element.14), channel_id=1, source_target_pairs={{16,32},{32,16},{48,64},{64,48},{80,96},{96,80},{112,128},{128,112... | collective-permute-start | bytes 282632 | tf_op jit(solution)/shard_map/ppermute | solution.py:23

commit v3 on v2

v3 whole, which is shorter than its diff:
```python
import jax
import jax.numpy as jnp
from jax import lax
from jax.experimental import pallas as pl
from jax.experimental.pallas import tpu as pltpu
from jax.sharding import PartitionSpec as P

HALF = 20
STEPS = 6
NEAR = 2
F32, BF16 = jnp.float32, jnp.bfloat16
VMEM = pl.BlockSpec(memory_space=pltpu.VMEM)
HBM = pl.BlockSpec(memory_space=pltpu.HBM)


def pairing(value, axis, offset):
    count = lax.axis_size(axis)
    pairs = []
    for i in range(count):
        other = ((i + offset) ^ 1) - offset
        if 0 <= other < count:
            pairs.append((i, other))
    return lax.ppermute(value, axis, pairs)


def low_part(value):
    return value - value.astype(BF16).astype(F32)


def pieces_x(nv, nc):
    spans, start = {}, 0
    for v in range(nv):
        spans["u", v], start = start, start + STEPS
    for c in range(nc):
        spans["t", c], start = start, start + STEPS
    for v in range(nv):
        spans["low", v], start = start, start + NEAR
    return spans, start


def pieces_z(nv, nc, nx):
    wide = nx + 2 * STEPS
    spans, start = {}, 0
    for d in range(STEPS):
        for v in range(nv):
            spans["u", v, d], start = start, start + wide
        for c in range(nc):
            spans["t", c, d], start = start, start + wide
    for d in range(NEAR):
        for v in range(nv):
            spans["low", v, d], start = start, start + nx
    return spans, start


def padded(rows):
    return -(-rows // 16) * 16


def parity(axis):
    return lax.rem(lax.axis_index(axis), 2)


def put_matrix(w, line, out):
    nt = line.shape[1]
    line[...] = jnp.zeros_like(line)
    line[0:1, 0 : w.shape[1]] = w[...]
    middle = pltpu.roll(line[...], nt - HALF, 1)
    source = lax.broadcasted_iota(jnp.int32, (nt, nt), 0)
    target = lax.broadcasted_iota(jnp.int32, (nt, nt), 1)
    band = pltpu.roll(jnp.broadcast_to(middle[0:1, :], (nt, nt)), 0, 1, stride=1, stride_axis=0)
    band = jnp.where(jnp.abs(target - source) <= HALF, band, 0.0)
    full = -0.25 * lax.dot_general(band, band, (((1,), (1,)), ((), ())), precision=lax.Precision.HIGHEST)
    full = jnp.where(source == target, 1.0 + full, full)
    high = full.astype(BF16)
    out[0:nt, 0:nt] = high
    out[nt : 2 * nt, 0:nt] = high
    out[0:nt, nt : 2 * nt] = (full - high.astype(F32)).astype(BF16)
    out[nt : 2 * nt, nt : 2 * nt] = jnp.zeros((nt, nt), BF16)


def pieces_o(nv, nc):
    names = [("u", v, d) for d in range(STEPS) for v in range(nv)]
    names += [("low", v, d) for d in range(NEAR) for v in range(nv)]
    names += [("t", c, d) for c in range(nc) for d in range(STEPS)]
    return {name: k for k, name in enumerate(names)}


def pack_x(probes, diffusion, wavelet):
    nv, ni, nx, nt = probes.shape
    nc = diffusion.shape[0]
    spans, each = pieces_x(nv, nc)
    o_pieces = pieces_o(nv, nc)
    rows = ni * each

    def kernel(u_hbm, t_hbm, w_hbm, even_ref, odd_ref, o_ref, u, t, g, stage, w, line, sems):
        taps = pltpu.make_async_copy(w_hbm, w, sems.at[nv + nc])
        taps.start()
        copies = []
        for source, target in ((u_hbm, u), (t_hbm, t)):
            for k in range(source.shape[0]):
                copies.append(pltpu.make_async_copy(source.at[k], target.at[k], sems.at[len(copies)]))
        for copy in copies:
            copy.start()
        taps.wait()
        put_matrix(w, line, g)
        for copy in copies:
            copy.wait()
        for side in range(2):
            first = 0 if side == 0 else nx - STEPS
            near = 0 if side == 0 else nx - NEAR
            tile = 0 if side == 0 else nx - 8
            for r in range(ni):
                base = r * each
                for v in range(nv):
                    start = base + spans["u", v]
                    stage[side, start : start + STEPS, :] = u[v, r, first : first + STEPS, :]
                    start = base + spans["low", v]
                    stage[side, start : start + NEAR, :] = low_part(u[v, r, near : near + NEAR, :])
                for c in range(nc):
                    start = base + spans["t", c]
                    edge = t[c, r, tile : tile + 8, :].astype(F32)
                    stage[side, start : start + STEPS, :] = edge[first - tile : first - tile + STEPS]
        odd = parity("xline")
        even_ref[...] = stage[1 - odd].astype(BF16)
        odd_ref[...] = stage[odd].astype(BF16)

        odd = parity("inline")
        edge, near = odd * (ni - STEPS), odd * (STEPS - NEAR)
        for d in range(STEPS):
            for v in range(nv):
                at = o_pieces["u", v, d] * nx
                o_ref[at : at + nx, :] = u[v, edge + d].astype(BF16)
            for c in range(nc):
                at = o_pieces["t", c, d] * nx
                o_ref[at : at + nx, :] = t[c, edge + d]
        for d in range(NEAR):
            for v in range(nv):
                at = o_pieces["low", v, d] * nx
                o_ref[at : at + nx, :] = low_part(u[v, edge + near + d]).astype(BF16)

    out = jax.ShapeDtypeStruct((rows, nt), BF16)
    return pl.pallas_call(
        kernel,
        out_shape=(
            out,
            out,
            jax.ShapeDtypeStruct((len(o_pieces) * nx, nt), BF16),
            jax.ShapeDtypeStruct(probes.shape, F32),
            jax.ShapeDtypeStruct(diffusion.shape, BF16),
            jax.ShapeDtypeStruct((2 * nt, 2 * nt), BF16),
        ),
        in_specs=[HBM] * 3,
        out_specs=(VMEM,) * 6,
        scratch_shapes=[
            pltpu.VMEM((2, rows, nt), F32),
            pltpu.VMEM((1, wavelet.shape[0]), F32),
            pltpu.VMEM((8, nt), F32),
            pltpu.SemaphoreType.DMA((nv + nc + 1,)),
        ],
        compiler_params=pltpu.CompilerParams(vmem_limit_bytes=4 << 20),
        name="pack_x",
    )(*(pltpu.with_memory_space_constraint(x, pltpu.HBM) for x in (probes, diffusion, wavelet.reshape(1, -1))))


def pack_z(probes, diffusion, even_x, odd_x):
    nv, ni, nx, nt = probes.shape
    nc = diffusion.shape[0]
    x_spans, x_each = pieces_x(nv, nc)
    spans, used = pieces_z(nv, nc, nx)
    corners, c_used = pieces_z(nv, nc, 0)
    rows, c_rows = padded(used), padded(c_used)

    def kernel(u, t, even_x_ref, odd_x_ref, e_ref, c_ref, halo, stage, stage_c):
        odd = parity("xline")
        halo[1 - odd] = even_x_ref[...].astype(F32)
        halo[odd] = odd_x_ref[...].astype(F32)
        for side in range(2):
            if rows > used:
                stage[side, used:rows, :] = jnp.zeros((rows - used, nt), F32)
            if c_rows > c_used:
                stage_c[side, c_used:c_rows, :] = jnp.zeros((c_rows - c_used, nt), F32)
            for d in range(STEPS):
                r = d if side == 0 else ni - STEPS + d
                for kind, count, ref in (("u", nv, u), ("t", nc, t)):
                    for k in range(count):
                        start = spans[kind, k, d]
                        at = r * x_each + x_spans[kind, k]
                        on_left, on_right = halo[0, at : at + STEPS, :], halo[1, at : at + STEPS, :]
                        stage[side, start : start + STEPS, :] = on_left
                        stage[side, start + STEPS : start + STEPS + nx, :] = ref[k, r, :, :].astype(F32)
                        stage[side, start + STEPS + nx : start + 2 * STEPS + nx, :] = on_right
                        start = corners[kind, k, d]
                        stage_c[side, start : start + STEPS, :] = on_left
                        stage_c[side, start + STEPS : start + 2 * STEPS, :] = on_right
            for d in range(NEAR):
                r = d if side == 0 else ni - NEAR + d
                for v in range(nv):
                    start = spans["low", v, d]
                    stage[side, start : start + nx, :] = low_part(u[v, r, :, :])
        odd = parity("inline")
        c_ref[...] = stage_c[odd].astype(BF16)
        e_ref[...] = stage[1 - odd].astype(BF16)

    return pl.pallas_call(
        kernel,
        out_shape=(jax.ShapeDtypeStruct((rows, nt), BF16), jax.ShapeDtypeStruct((c_rows, nt), BF16)),
        in_specs=[VMEM] * 4,
        out_specs=(VMEM, VMEM),
        scratch_shapes=[
            pltpu.VMEM((2, ni * x_each, nt), F32),
            pltpu.VMEM((2, rows, nt), F32),
            pltpu.VMEM((2, c_rows, nt), F32),
        ],
        compiler_params=pltpu.CompilerParams(vmem_limit_bytes=8 << 20),
        name="pack_z",
    )(probes, diffusion, even_x, odd_x)


EDGE = 8


def lay_out(probes, diffusion, even_x, odd_x):
    nv, ni, nx, nt = probes.shape
    nc = diffusion.shape[0]
    spans, each = pieces_x(nv, nc)
    height, width = ni + 2 * STEPS, nx + 3 * EDGE

    def kernel(u0, t0, even_ref, odd_ref, u, t, halo):
        odd = parity("xline")
        halo[1 - odd] = even_ref[...].astype(F32)
        halo[odd] = odd_ref[...].astype(F32)
        for v in range(nv):
            u[v, STEPS : STEPS + ni, EDGE : EDGE + nx, :] = u0[v]
        for c in range(nc):
            t[c, STEPS : STEPS + ni, EDGE : EDGE + nx, :] = 0.25 * t0[c].astype(F32)
        for r in range(ni):
            e, base = r + STEPS, r * each
            for side, first, near in ((0, EDGE - STEPS, STEPS - NEAR), (1, EDGE + nx, 0)):
                for v in range(nv):
                    at, low = base + spans["u", v], base + spans["low", v]
                    u[v, e, first : first + STEPS, :] = halo[side, at : at + STEPS, :]
                    u[v, e, first + near : first + near + NEAR, :] = (
                        halo[side, at + near : at + near + NEAR, :] + halo[side, low : low + NEAR, :]
                    )
                for c in range(nc):
                    at = base + spans["t", c]
                    t[c, e, first : first + STEPS, :] = 0.25 * halo[side, at : at + STEPS, :]

    return pl.pallas_call(
        kernel,
        out_shape=(
            jax.ShapeDtypeStruct((nv, height + STEPS, width, nt), F32),
            jax.ShapeDtypeStruct((nc, height, width, nt), F32),
        ),
        in_specs=[VMEM] * 4,
        out_specs=(VMEM, VMEM),
        scratch_shapes=[pltpu.VMEM((2, ni * each, nt), F32)],
        compiler_params=pltpu.CompilerParams(vmem_limit_bytes=4 << 20),
        cost_estimate=pl.CostEstimate(flops=1 << 20, bytes_accessed=4 << 20, transcendentals=0),
        name="lay_out",
    )(probes, diffusion, even_x, odd_x)


def take_rows(first, high_side, message, halo, u, t, nx):
    spans, _ = pieces_z(u.shape[0], t.shape[0], nx)
    halo[...] = message[...].astype(F32)
    left, wide = EDGE - STEPS, nx + 2 * STEPS
    near = 0 if high_side else STEPS - NEAR
    for d in range(STEPS):
        for v in range(u.shape[0]):
            at = spans["u", v, d]
            u[v, first + d, left : left + wide, :] = halo[at : at + wide, :]
        for c in range(t.shape[0]):
            at = spans["t", c, d]
            t[c, first + d, left : left + wide, :] = 0.25 * halo[at : at + wide, :]
    for d in range(NEAR):
        for v in range(u.shape[0]):
            at, e = spans["low", v, d], first + near + d
            u[v, e, EDGE : EDGE + nx, :] = u[v, e, EDGE : EDGE + nx, :] + halo[at : at + nx, :]


def take_split_rows(first, high_side, rows, corners, halo, u, t, nx):
    spans, _ = pieces_z(u.shape[0], t.shape[0], 0)
    pieces = pieces_o(u.shape[0], t.shape[0])
    halo[...] = corners[...].astype(F32)
    near = 0 if high_side else STEPS - NEAR
    for d in range(STEPS):
        for kind, ref, scale in (("u", u, 1.0), ("t", t, 0.25)):
            for k in range(ref.shape[0]):
                at = spans[kind, k, d]
                ref[k, first + d, EDGE - STEPS : EDGE, :] = scale * halo[at : at + STEPS, :]
                ref[k, first + d, EDGE + nx : EDGE + nx + STEPS, :] = scale * halo[at + STEPS : at + 2 * STEPS, :]
                at = pieces[kind, k, d] * nx
                whole = rows[at : at + nx, :].astype(F32)
                if kind == "u" and near <= d < near + NEAR:
                    at = pieces["low", k, d - near] * nx
                    whole = whole + rows[at : at + nx, :].astype(F32)
                ref[k, first + d, EDGE : EDGE + nx, :] = scale * whole


def advance(step, first, count, above, below, refs, inside_x, inside_in, beyond, nx):
    u, t, g, data, cross = refs
    nv, nt = u.shape[0], u.shape[3]
    start, wide = (2, nx + 16) if step <= 2 else (4, nx + 8)
    window = slice(start, start + wide)
    tiles = [slice(at, at + TILE) for at in range(start, start + wide, TILE)]
    right_of = lambda cols: slice(cols.start + 1, cols.stop + 1)
    keeps = {}
    for cols in tiles:
        if cols.stop > EDGE + nx:
            column = lax.broadcasted_iota(jnp.int32, (TILE, nt), 0) + cols.start
            keeps[cols.start] = jnp.logical_or(column < EDGE + nx, inside_x)
    before = {}
    last = first + count
    for low in range(first, last, CHUNK):
        high = min(low + CHUNK, last)
        rows = nv * (high - low) * wide
        block = u[:, low:high, window, :].reshape(rows, nt)
        upper = block.astype(BF16)
        lower = (block - upper.astype(F32)).astype(BF16)
        both = jnp.dot(jnp.concatenate([upper, lower], axis=1), g, preferred_element_type=F32)
        data[0:rows, :] = both[:, 0:nt] + both[:, nt : 2 * nt]
        for cols in tiles:
            right = right_of(cols)
            for v in range(nv):
                if low == first:
                    here = u[v, above, cols, :]
                    a, b = t[0, first - 1, cols, :], t[1, first - 1, cols, :]
                    before[v, cols.start] = a * (u[v, first, cols, :] - here) + b * (u[v, above, right, :] - here)
            for e in range(low, high):
                after = below if e == last - 1 else e + 1
                a, b, c = t[0, e, cols, :], t[1, e, cols, :], t[2, e, cols, :]
                for v in range(nv):
                    here = u[v, e, cols, :]
                    step_in = u[v, after, cols, :] - here
                    step_x = u[v, e, right, :] - here
                    flux_in = a * step_in + b * step_x
                    flux_x = b * step_in + c * step_x
                    slot, at = (e - low) * nv + v, 8 + cols.start - start
                    cross[slot, at : at + TILE, :] = flux_x
                    turn = (flux_in - before[v, cols.start]) + (flux_x - cross[slot, at - 1 : at - 1 + TILE, :])
                    at = (v * (high - low) + e - low) * wide + cols.start - start
                    renewed = data[at : at + TILE, :] + turn
                    before[v, cols.start] = flux_in
                    if e >= beyond:
                        renewed = jnp.where(inside_in, renewed, 0.0)
                    if cols.start in keeps:
                        renewed = jnp.where(keeps[cols.start], renewed, 0.0)
                    u[v, e, cols, :] = renewed


TILE = 8
CHUNK = 20


def sweep_scratch(message_rows, nv, nx, nt):
    return [
        pltpu.VMEM((message_rows, nt), F32),
        pltpu.VMEM((nv * CHUNK * (nx + 16), nt), F32),
        pltpu.VMEM((CHUNK * nv, nx + 24, nt), F32),
    ]


def inner(axis):
    return lax.axis_index(axis) < lax.axis_size(axis) - 1


def sweep_far(u, t, message, matrix, ni, nx):
    nv, _, _, nt = u.shape
    height = ni + 2 * STEPS

    def kernel(u_in, t_in, message_ref, g_ref, u, t, halo, data, cross):
        inside_x = inner("xline")
        refs = (u, t, g_ref[...], data, cross)

        def run(odd):
            take_rows(0 if odd else STEPS + ni, not odd, message_ref, halo, u, t, nx)
            for step in range(1, STEPS + 1):
                first = step if odd else STEPS + step
                count = ni + STEPS - 2 * step
                border = first + count - 1 if odd else first
                for v in range(nv):
                    u[v, height + step - 1] = u[v, border]
                advance(step, first, count, first - 1, first + count, refs, inside_x, None, height, nx)

        odd = parity("inline")
        pl.when(odd == 0)(lambda: run(False))
        pl.when(odd == 1)(lambda: run(True))

    return pl.pallas_call(
        kernel,
        out_shape=(jax.ShapeDtypeStruct(u.shape, F32), jax.ShapeDtypeStruct(t.shape, F32)),
        in_specs=[VMEM] * 4,
        out_specs=(VMEM, VMEM),
        input_output_aliases={0: 0, 1: 1},
        scratch_shapes=sweep_scratch(message.shape[0], nv, nx, nt),
        compiler_params=pltpu.CompilerParams(vmem_limit_bytes=8 << 20),
        cost_estimate=pl.CostEstimate(flops=1 << 28, bytes_accessed=16 << 20, transcendentals=0),
        name="sweep_far",
    )(u, t, message, matrix)


def sweep_near(u, t, message, corners, matrix, ni, nx):
    nv, _, _, nt = u.shape
    height = ni + 2 * STEPS

    def kernel(u_in, t_in, message_ref, corners_ref, g_ref, out_hbm, u, t, halo, data, cross, sems):
        inside_x, inside_in = inner("xline"), inner("inline")
        refs = (u, t, g_ref[...], data, cross)

        def result(row, count, k):
            source = u.at[:, pl.ds(STEPS + row, count), pl.ds(EDGE, nx), :]
            return pltpu.make_async_copy(source, out_hbm.at[:, pl.ds(row, count), :, :], sems.at[k])

        def run(odd):
            ready = result(0 if odd else STEPS, ni - STEPS, 0)
            ready.start()
            take_split_rows(STEPS + ni if odd else 0, odd, message_ref, corners_ref, halo, u, t, nx)
            for step in range(1, STEPS + 1):
                first = STEPS + ni - step if odd else step
                kept = height + step - 1
                above = kept if odd else first - 1
                below = first + STEPS if odd else kept
                advance(step, first, STEPS, above, below, refs, inside_x, inside_in, STEPS + ni if odd else height, nx)
            rest = result(ni - STEPS if odd else 0, STEPS, 1)
            rest.start()
            ready.wait()
            rest.wait()

        odd = parity("inline")
        pl.when(odd == 0)(lambda: run(False))
        pl.when(odd == 1)(lambda: run(True))

    out = pl.pallas_call(
        kernel,
        out_shape=(
            jax.ShapeDtypeStruct((nv, ni, nx, nt), F32),
            jax.ShapeDtypeStruct(u.shape, F32),
            jax.ShapeDtypeStruct(t.shape, F32),
        ),
        in_specs=[VMEM] * 5,
        out_specs=(HBM, VMEM, VMEM),
        input_output_aliases={0: 1, 1: 2},
        scratch_shapes=sweep_scratch(corners.shape[0], nv, nx, nt) + [pltpu.SemaphoreType.DMA((2,))],
        compiler_params=pltpu.CompilerParams(vmem_limit_bytes=8 << 20),
        name="sweep_near",
    )(u, t, message, corners, matrix)
    return out[0]


def per_device(probes, diffusion, wavelet):
    _, ni, nx, _ = probes.shape
    even_x, odd_x, o_rows, probes, diffusion, matrix = pack_x(probes, diffusion, wavelet)
    odd_x = pairing(odd_x, "xline", 1)
    even_x = pairing(even_x, "xline", 0)
    o_rows = pairing(o_rows, "inline", 1)
    e_rows, corners = pack_z(probes, diffusion, even_x, odd_x)
    e_rows = pairing(e_rows, "inline", 0)
    corners = pairing(corners, "inline", 1)
    u, t = lay_out(probes, diffusion, even_x, odd_x)
    u, t = sweep_far(u, t, e_rows, matrix, ni, nx)
    return sweep_near(u, t, o_rows, corners, matrix, ni, nx)


def solution(mesh):
    return jax.shard_map(
        per_device,
        mesh=mesh,
        in_specs=(P(None, "inline", "xline", None), P(None, "inline", "xline", None), P()),
        out_specs=P(None, "inline", "xline", None),
        check_vma=False,
    )
```

time: 36.4 us -> 31.1 us (0.85)
  waiting for transfers between devices: 9.25 us -> 5.59 us
  Pallas kernels: 9.2 us -> 7.67 us
    ppermute x5, waiting for transfers between devices: 9.25 us -> 5.59 us  [pairing(): return lax.ppermute(value, axis, pairs)]
    pallas_call x3 -> x4, Pallas kernels: 8.97 us -> 7.44 us  [the longest x1 3.62 us: sweep_far(): pl.pallas_call(kernel, out_shape=(jax.ShapeDtypeStruct(u.shape, F32), jax...]
  transfers between devices with their start and end apart: 5 -> 5, of which waited for: 2 -> 2; matrix products, arithmetic and copies ran while one was open for 0% -> 0% of each run, Pallas kernels for 1% -> 12%
where the time goes in v3:
time: 31.1 us; the launch traced here: 30.8 us
  starting transfers between devices  17.5 us (56%)
  Pallas kernels  7.67 us (25%)
  waiting for transfers between devices  5.59 us (18%)
    ppermute x5, starting transfers between devices, pairing(): return lax.ppermute(value, axis, pairs)  17.5 us
    ppermute x5, waiting for transfers between devices, pairing(): return lax.ppermute(value, axis, pairs)  5.59 us
    pallas_call x1, Pallas kernels, sweep_far(): pl.pallas_call(kernel, out_shape=(jax.ShapeDtypeStruct(u.shape, F32), jax...  3.62 us
    pallas_call x1, Pallas kernels, sweep_near(): pl.pallas_call(kernel, out_shape=(jax.ShapeDtypeStruct((nv, ni, nx, nt),...  2.24 us
    pallas_call x1, Pallas kernels, pack_x(): pl.pallas_call(kernel, out_shape=(out, out, jax.ShapeDtypeStruct((len(o_p...  1.35 us
  transfers between devices with their start and end apart: 5, of which 2 were waited for; matrix products, arithmetic and copies ran while one was open for 0% of the time, Pallas kernels for 12%

profile of v3, /device:TPU:227, one launch (start us, length us, event | category | flops | bytes accessed | tf_op | source)
XLA Modules:
  0.0 30.8 jit_solution(15639271186963463242)
XLA Ops:
  0.0 1.4 %pack_x.1 = (bf16[544,128]{1,0:T(8,128)(2,1)S(1)}, bf16[544,128]{1,0:T(8,128)(2,1)S(1)}, bf16[1088,128]{1,0:T(8,128)(2,1)S(1)}, f32[2,16,32,128]{3,2,1,0:T(8,128...) custom-call(f32[2,16,32,128]{3,2,1,0:T(8,128)} %u_hbm.1, bf16[3,16,32,128]{3,2,1,0:T(8,128)(2,1)} %t_hbm.1, ...), custom_call_target="tpu_custom_call" | custom-call | tf_op jit(solution)/shard_map/pack_x/pallas_call | solution.py:142
  1.4 3.2 %collective-permute-start = (bf16[544,128]{1,0:T(8,128)(2,1)S(1)}, bf16[544,128]{1,0:T(8,128)(2,1)S(1)}, u32[]{:S(2)}, u32[]{:S(2)}) collective-permute-start(bf16[544,128]{1,0:T(8,128)(2,1)S(1)} %get-tuple-element.20), channel_id=1, source_target_pairs={{0,1},{1,0},{2,3},{3,2},{4,5},{5,4},{6,7},{7,6},{8,9},{9,8},{10,11... | collective-permute-start | bytes 417800 | tf_op jit(solution)/shard_map/ppermute | solution.py:23
  4.6 3.8 %collective-permute-start.1 = (bf16[544,128]{1,0:T(8,128)(2,1)S(1)}, bf16[544,128]{1,0:T(8,128)(2,1)S(1)}, u32[]{:S(2)}, u32[]{:S(2)}) collective-permute-start(bf16[544,128]{1,0:T(8,128)(2,1)S(1)} %get-tuple-element.21), channel_id=1, source_target_pairs={{1,2},{2,1},{3,4},{4,3},{5,6},{6,5},{7,8},{8,7},{9,10},{10,9},{11,... | collective-permute-start | bytes 417800 | tf_op jit(solution)/shard_map/ppermute | solution.py:23
  8.4 0.0 collective-permute-done.even_ref.even_x_ref
  8.4 4.5 %collective-permute-done.1.odd_ref.odd_x_ref = bf16[544,128]{1,0:T(8,128)(2,1)S(1)} collective-permute-done((bf16[544,128]{1,0:T(8,128)(2,1)S(1)}, bf16[544,128]{1,0:T(8,128)(2,1)S(1)}, u32[]{:S(2)}, u32[]{:S(2)}) %collective-permute-start.1) | collective-permute-done | bytes 139296 | tf_op jit(solution)/shard_map/ppermute | solution.py:23
  12.9 0.2 pack_z.1
  13.1 3.7 %collective-permute-start.2 = (bf16[1456,128]{1,0:T(8,128)(2,1)S(1)}, bf16[1456,128]{1,0:T(8,128)(2,1)S(1)}, u32[]{:S(2)}, u32[]{:S(2)}) collective-permute-start(bf16[1456,128]{1,0:T(8,128)(2,1)S(1)} %get-tuple-element.24), channel_id=1, source_target_pairs={{0,16},{16,0},{32,48},{48,32},{64,80},{80,64},{96,112},{112,96},{1... | collective-permute-start | bytes 1118216 | tf_op jit(solution)/shard_map/ppermute | solution.py:23
  16.8 4.7 %collective-permute-start.3 = (bf16[1088,128]{1,0:T(8,128)(2,1)S(1)}, bf16[1088,128]{1,0:T(8,128)(2,1)S(1)}, u32[]{:S(2)}, u32[]{:S(2)}) collective-permute-start(bf16[1088,128]{1,0:T(8,128)(2,1)S(1)} %get-tuple-element.28), channel_id=1, source_target_pairs={{16,32},{32,16},{48,64},{64,48},{80,96},{96,80},{112,128},{128,112... | collective-permute-start | bytes 835592 | tf_op jit(solution)/shard_map/ppermute | solution.py:23
  21.5 2.1 %collective-permute-start.4 = (bf16[368,128]{1,0:T(8,128)(2,1)S(1)}, bf16[368,128]{1,0:T(8,128)(2,1)S(1)}, u32[]{:S(2)}, u32[]{:S(2)}) collective-permute-start(bf16[368,128]{1,0:T(8,128)(2,1)S(1)} %get-tuple-element.29), channel_id=1, source_target_pairs={{16,32},{32,16},{48,64},{64,48},{80,96},{96,80},{112,128},{128,112... | collective-permute-start | bytes 282632 | tf_op jit(solution)/shard_map/ppermute | solution.py:23
  23.6 0.2 lay_out.1
  23.8 0.0 collective-permute-done.2.message_ref
  23.8 3.6 %sweep_far.1 = (f32[2,34,56,128]{3,2,1,0:T(8,128)S(1)}, f32[3,28,56,128]{3,2,1,0:T(8,128)S(1)}) custom-call(f32[2,34,56,128]{3,2,1,0:T(8,128)S(1)} %get-tuple-element.22.u_in, f32[3,28,56,128]{3,2,1,0:T(8,128)S(1)} %get-tuple-element.23.t_in, bf16[1456,128]{1,0:T(8,128)(2,1)S(1)} %collective-permute-done.2.message_ref, ...), custom_call_target="tpu_custom_call", output_to_operand_aliasing={{0}: (0, {}), {1}: (1, {})} | custom-call | flops 268435456 | bytes 16777216 | tf_op jit(solution)/shard_map/sweep_far/pallas_call | solution.py:390
  27.5 1.1 %collective-permute-done.4.corners_ref = bf16[368,128]{1,0:T(8,128)(2,1)S(1)} collective-permute-done((bf16[368,128]{1,0:T(8,128)(2,1)S(1)}, bf16[368,128]{1,0:T(8,128)(2,1)S(1)}, u32[]{:S(2)}, u32[]{:S(2)}) %collective-permute-start.4) | collective-permute-done | bytes 94240 | tf_op jit(solution)/shard_map/ppermute | solution.py:23
  28.6 0.0 collective-permute-done.3.message_ref
  28.6 2.2 %sweep_near.1 = (f32[2,16,32,128]{3,2,1,0:T(8,128)}, f32[2,34,56,128]{3,2,1,0:T(8,128)S(1)}, f32[3,28,56,128]{3,2,1,0:T(8,128)S(1)}) custom-call(f32[2,34,56,128]{3,2,1,0:T(8,128)S(1)} %get-tuple-element.26.u_in, f32[3,28,56,128]{3,2,1,0:T(8,128)S(1)} %get-tuple-element.27.t_in, ...), custom_call_target="tpu_custom_call", output_to_operand_aliasing={{1}: (0, {}), {2}: (1, {})} | custom-call | tf_op jit(solution)/shard_map/sweep_near/pallas_call | solution.py:434
Async XLA Ops:
  1.4 7.0 %collective-permute-start = (bf16[544,128]{1,0:T(8,128)(2,1)S(1)}, bf16[544,128]{1,0:T(8,128)(2,1)S(1)}, u32[]{:S(2)}, u32[]{:S(2)}) collective-permute-start(bf16[544,128]{1,0:T(8,128)(2,1)S(1)} %get-tuple-element.20), channel_id=1, source_target_pairs={{0,1},{1,0},{2,3},{3,2},{4,5},{5,4},{6,7},{7,6},{8,9},{9,8},{10,11... | collective-permute-start | bytes 417800 | tf_op jit(solution)/shard_map/ppermute | solution.py:23
  4.6 8.3 %collective-permute-start.1 = (bf16[544,128]{1,0:T(8,128)(2,1)S(1)}, bf16[544,128]{1,0:T(8,128)(2,1)S(1)}, u32[]{:S(2)}, u32[]{:S(2)}) collective-permute-start(bf16[544,128]{1,0:T(8,128)(2,1)S(1)} %get-tuple-element.21), channel_id=1, source_target_pairs={{1,2},{2,1},{3,4},{4,3},{5,6},{6,5},{7,8},{8,7},{9,10},{10,9},{11,... | collective-permute-start | bytes 417800 | tf_op jit(solution)/shard_map/ppermute | solution.py:23
  13.1 10.8 %collective-permute-start.2 = (bf16[1456,128]{1,0:T(8,128)(2,1)S(1)}, bf16[1456,128]{1,0:T(8,128)(2,1)S(1)}, u32[]{:S(2)}, u32[]{:S(2)}) collective-permute-start(bf16[1456,128]{1,0:T(8,128)(2,1)S(1)} %get-tuple-element.24), channel_id=1, source_target_pairs={{0,16},{16,0},{32,48},{48,32},{64,80},{80,64},{96,112},{112,96},{1... | collective-permute-start | bytes 1118216 | tf_op jit(solution)/shard_map/ppermute | solution.py:23
  16.8 11.8 %collective-permute-start.3 = (bf16[1088,128]{1,0:T(8,128)(2,1)S(1)}, bf16[1088,128]{1,0:T(8,128)(2,1)S(1)}, u32[]{:S(2)}, u32[]{:S(2)}) collective-permute-start(bf16[1088,128]{1,0:T(8,128)(2,1)S(1)} %get-tuple-element.28), channel_id=1, source_target_pairs={{16,32},{32,16},{48,64},{64,48},{80,96},{96,80},{112,128},{128,112... | collective-permute-start | bytes 835592 | tf_op jit(solution)/shard_map/ppermute | solution.py:23
  21.5 7.1 %collective-permute-start.4 = (bf16[368,128]{1,0:T(8,128)(2,1)S(1)}, bf16[368,128]{1,0:T(8,128)(2,1)S(1)}, u32[]{:S(2)}, u32[]{:S(2)}) collective-permute-start(bf16[368,128]{1,0:T(8,128)(2,1)S(1)} %get-tuple-element.29), channel_id=1, source_target_pairs={{16,32},{32,16},{48,64},{64,48},{80,96},{96,80},{112,128},{128,112... | collective-permute-start | bytes 282632 | tf_op jit(solution)/shard_map/ppermute | solution.py:23

commit v4 on v3

--- a/solution.py
+++ b/solution.py
@@ -93,17 +93,20 @@
     rows = ni * each
 
     def kernel(u_hbm, t_hbm, w_hbm, even_ref, odd_ref, o_ref, u, t, g, stage, w, line, sems):
-        taps = pltpu.make_async_copy(w_hbm, w, sems.at[nv + nc])
+        taps = pltpu.make_async_copy(w_hbm, w, sems.at[6])
         taps.start()
-        copies = []
-        for source, target in ((u_hbm, u), (t_hbm, t)):
-            for k in range(source.shape[0]):
-                copies.append(pltpu.make_async_copy(source.at[k], target.at[k], sems.at[len(copies)]))
-        for copy in copies:
+        edges, middle = [], []
+        for spans_of, copies in ((((0, 8), (nx - 8, 8)), edges), (((8, nx - 16),), middle)):
+            for first, count in spans_of:
+                for source, target in ((u_hbm, u), (t_hbm, t)):
+                    part = (slice(None), slice(None), pl.ds(first, count), slice(None))
+                    sem = sems.at[len(edges) + len(middle)]
+                    copies.append(pltpu.make_async_copy(source.at[part], target.at[part], sem))
+        for copy in edges + middle:
             copy.start()
         taps.wait()
         put_matrix(w, line, g)
-        for copy in copies:
+        for copy in edges:
             copy.wait()
         for side in range(2):
             first = 0 if side == 0 else nx - STEPS
@@ -124,6 +127,8 @@
         even_ref[...] = stage[1 - odd].astype(BF16)
         odd_ref[...] = stage[odd].astype(BF16)
 
+        for copy in middle:
+            copy.wait()
         odd = parity("inline")
         edge, near = odd * (ni - STEPS), odd * (STEPS - NEAR)
         for d in range(STEPS):
@@ -155,7 +160,7 @@
             pltpu.VMEM((2, rows, nt), F32),
             pltpu.VMEM((1, wavelet.shape[0]), F32),
             pltpu.VMEM((8, nt), F32),
-            pltpu.SemaphoreType.DMA((nv + nc + 1,)),
+            pltpu.SemaphoreType.DMA((7,)),
         ],
         compiler_params=pltpu.CompilerParams(vmem_limit_bytes=4 << 20),
         name="pack_x",
@@ -219,46 +224,29 @@
 EDGE = 8
 
 
-def lay_out(probes, diffusion, even_x, odd_x):
-    nv, ni, nx, nt = probes.shape
-    nc = diffusion.shape[0]
+def lay_out(u0, t0, even_ref, odd_ref, u, t, halo):
+    nv, ni, nx, _ = u0.shape
+    nc = t0.shape[0]
     spans, each = pieces_x(nv, nc)
-    height, width = ni + 2 * STEPS, nx + 3 * EDGE
-
-    def kernel(u0, t0, even_ref, odd_ref, u, t, halo):
-        odd = parity("xline")
-        halo[1 - odd] = even_ref[...].astype(F32)
-        halo[odd] = odd_ref[...].astype(F32)
-        for v in range(nv):
-            u[v, STEPS : STEPS + ni, EDGE : EDGE + nx, :] = u0[v]
-        for c in range(nc):
-            t[c, STEPS : STEPS + ni, EDGE : EDGE + nx, :] = 0.25 * t0[c].astype(F32)
-        for r in range(ni):
-            e, base = r + STEPS, r * each
-            for side, first, near in ((0, EDGE - STEPS, STEPS - NEAR), (1, EDGE + nx, 0)):
-                for v in range(nv):
-                    at, low = base + spans["u", v], base + spans["low", v]
-                    u[v, e, first : first + STEPS, :] = halo[side, at : at + STEPS, :]
-                    u[v, e, first + near : first + near + NEAR, :] = (
-                        halo[side, at + near : at + near + NEAR, :] + halo[side, low : low + NEAR, :]
-                    )
-                for c in range(nc):
-                    at = base + spans["t", c]
-                    t[c, e, first : first + STEPS, :] = 0.25 * halo[side, at : at + STEPS, :]
-
-    return pl.pallas_call(
-        kernel,
-        out_shape=(
-            jax.ShapeDtypeStruct((nv, height + STEPS, width, nt), F32),
-            jax.ShapeDtypeStruct((nc, height, width, nt), F32),
-        ),
-        in_specs=[VMEM] * 4,
-        out_specs=(VMEM, VMEM),
-        scratch_shapes=[pltpu.VMEM((2, ni * each, nt), F32)],
-        compiler_params=pltpu.CompilerParams(vmem_limit_bytes=4 << 20),
-        cost_estimate=pl.CostEstimate(flops=1 << 20, bytes_accessed=4 << 20, transcendentals=0),
-        name="lay_out",
-    )(probes, diffusion, even_x, odd_x)
+    odd = parity("xline")
+    halo[1 - odd] = even_ref[...].astype(F32)
+    halo[odd] = odd_ref[...].astype(F32)
+    for v in range(nv):
+        u[v, STEPS : STEPS + ni, EDGE : EDGE + nx, :] = u0[v]
+    for c in range(nc):
+        t[c, STEPS : STEPS + ni, EDGE : EDGE + nx, :] = 0.25 * t0[c].astype(F32)
+    for r in range(ni):
+        e, base = r + STEPS, r * each
+        for side, first, near in ((0, EDGE - STEPS, STEPS - NEAR), (1, EDGE + nx, 0)):
+            for v in range(nv):
+                at, low = base + spans["u", v], base + spans["low", v]
+                u[v, e, first : first + STEPS, :] = halo[side, at : at + STEPS, :]
+                u[v, e, first + near : first + near + NEAR, :] = (
+                    halo[side, at + near : at + near + NEAR, :] + halo[side, low : low + NEAR, :]
+                )
+            for c in range(nc):
+                at = base + spans["t", c]
+                t[c, e, first : first + STEPS, :] = 0.25 * halo[side, at : at + STEPS, :]
 
 
 def take_rows(first, high_side, message, halo, u, t, nx):
@@ -299,7 +287,7 @@
 
 
 def advance(step, first, count, above, below, refs, inside_x, inside_in, beyond, nx):
-    u, t, g, data, cross = refs
+    u, t, g, data, _ = refs
     nv, nt = u.shape[0], u.shape[3]
     start, wide = (2, nx + 16) if step <= 2 else (4, nx + 8)
     window = slice(start, start + wide)
@@ -320,26 +308,30 @@
         lower = (block - upper.astype(F32)).astype(BF16)
         both = jnp.dot(jnp.concatenate([upper, lower], axis=1), g, preferred_element_type=F32)
         data[0:rows, :] = both[:, 0:nt] + both[:, nt : 2 * nt]
-        for cols in tiles:
-            right = right_of(cols)
-            for v in range(nv):
-                if low == first:
+        top = lax.broadcasted_iota(jnp.int32, (TILE, nt), 0) == 0
+        if low == first:
+            for cols in tiles:
+                a, b = t[0, first - 1, cols, :], t[1, first - 1, cols, :]
+                for v in range(nv):
                     here = u[v, above, cols, :]
-                    a, b = t[0, first - 1, cols, :], t[1, first - 1, cols, :]
-                    before[v, cols.start] = a * (u[v, first, cols, :] - here) + b * (u[v, above, right, :] - here)
-            for e in range(low, high):
-                after = below if e == last - 1 else e + 1
+                    step_x = u[v, above, right_of(cols), :] - here
+                    before[v, cols.start] = a * (u[v, first, cols, :] - here) + b * step_x
+        for e in range(low, high):
+            after = below if e == last - 1 else e + 1
+            carried = [None] * nv
+            for cols in tiles:
                 a, b, c = t[0, e, cols, :], t[1, e, cols, :], t[2, e, cols, :]
                 for v in range(nv):
                     here = u[v, e, cols, :]
                     step_in = u[v, after, cols, :] - here
-                    step_x = u[v, e, right, :] - here
+                    step_x = u[v, e, right_of(cols), :] - here
                     flux_in = a * step_in + b * step_x
                     flux_x = b * step_in + c * step_x
-                    slot, at = (e - low) * nv + v, 8 + cols.start - start
-                    cross[slot, at : at + TILE, :] = flux_x
-                    turn = (flux_in - before[v, cols.start]) + (flux_x - cross[slot, at - 1 : at - 1 + TILE, :])
+                    turned = pltpu.roll(flux_x, 1, 0)
+                    shifted = turned if carried[v] is None else jnp.where(top, carried[v], turned)
+                    carried[v] = turned
                     at = (v * (high - low) + e - low) * wide + cols.start - start
+                    turn = (flux_in - before[v, cols.start]) + (flux_x - shifted)
                     renewed = data[at : at + TILE, :] + turn
                     before[v, cols.start] = flux_in
                     if e >= beyond:
@@ -365,13 +357,15 @@
     return lax.axis_index(axis) < lax.axis_size(axis) - 1
 
 
-def sweep_far(u, t, message, matrix, ni, nx):
-    nv, _, _, nt = u.shape
-    height = ni + 2 * STEPS
-
-    def kernel(u_in, t_in, message_ref, g_ref, u, t, halo, data, cross):
-        inside_x = inner("xline")
+def sweep_far(probes, diffusion, even_x, odd_x, message, matrix):
+    nv, ni, nx, nt = probes.shape
+    nc = diffusion.shape[0]
+    height, width = ni + 2 * STEPS, nx + 3 * EDGE
+
+    def kernel(u0, t0, even_ref, odd_ref, message_ref, g_ref, u, t, halo_x, halo, data, cross):
+        inside_x, inside_in = inner("xline"), None
         refs = (u, t, g_ref[...], data, cross)
+        lay_out(u0, t0, even_ref, odd_ref, u, t, halo_x)
 
         def run(odd):
             take_rows(0 if odd else STEPS + ni, not odd, message_ref, halo, u, t, nx)
@@ -381,7 +375,7 @@
                 border = first + count - 1 if odd else first
                 for v in range(nv):
                     u[v, height + step - 1] = u[v, border]
-                advance(step, first, count, first - 1, first + count, refs, inside_x, None, height, nx)
+                advance(step, first, count, first - 1, first + count, refs, inside_x, inside_in, height, nx)
 
         odd = parity("inline")
         pl.when(odd == 0)(lambda: run(False))
@@ -389,15 +383,17 @@
 
     return pl.pallas_call(
         kernel,
-        out_shape=(jax.ShapeDtypeStruct(u.shape, F32), jax.ShapeDtypeStruct(t.shape, F32)),
-        in_specs=[VMEM] * 4,
+        out_shape=(
+            jax.ShapeDtypeStruct((nv, height + STEPS, width, nt), F32),
+            jax.ShapeDtypeStruct((nc, height, width, nt), F32),
+        ),
+        in_specs=[VMEM] * 6,
         out_specs=(VMEM, VMEM),
-        input_output_aliases={0: 0, 1: 1},
-        scratch_shapes=sweep_scratch(message.shape[0], nv, nx, nt),
+        scratch_shapes=[pltpu.VMEM((2, even_x.shape[0], nt), F32)] + sweep_scratch(message.shape[0], nv, nx, nt),
         compiler_params=pltpu.CompilerParams(vmem_limit_bytes=8 << 20),
         cost_estimate=pl.CostEstimate(flops=1 << 28, bytes_accessed=16 << 20, transcendentals=0),
         name="sweep_far",
-    )(u, t, message, matrix)
+    )(probes, diffusion, even_x, odd_x, message, matrix)
 
 
 def sweep_near(u, t, message, corners, matrix, ni, nx):
@@ -457,8 +453,7 @@
     e_rows, corners = pack_z(probes, diffusion, even_x, odd_x)
     e_rows = pairing(e_rows, "inline", 0)
     corners = pairing(corners, "inline", 1)
-    u, t = lay_out(probes, diffusion, even_x, odd_x)
-    u, t = sweep_far(u, t, e_rows, matrix, ni, nx)
+    u, t = sweep_far(probes, diffusion, even_x, odd_x, e_rows, matrix)
     return sweep_near(u, t, o_rows, corners, matrix, ni, nx)
 
 

time: 31.1 us -> 30.8 us (level)
  the two profiles are of different devices: /device:TPU:227 before, /device:TPU:101 now
where the time goes in v4:
time: 30.8 us; the launch traced here: 30.6 us
  starting transfers between devices  17.5 us (57%)
  Pallas kernels  6.95 us (23%)
  waiting for transfers between devices  6.09 us (20%)
    ppermute x5, starting transfers between devices, pairing(): return lax.ppermute(value, axis, pairs)  17.5 us
    ppermute x5, waiting for transfers between devices, pairing(): return lax.ppermute(value, axis, pairs)  6.09 us
    pallas_call x1, Pallas kernels, sweep_far(): pl.pallas_call(kernel, out_shape=(jax.ShapeDtypeStruct((nv, height + STEP...  3.36 us
    pallas_call x1, Pallas kernels, sweep_near(): pl.pallas_call(kernel, out_shape=(jax.ShapeDtypeStruct((nv, ni, nx, nt),...  2.01 us
    pallas_call x1, Pallas kernels, pack_x(): pl.pallas_call(kernel, out_shape=(out, out, jax.ShapeDtypeStruct((len(o_p...  1.35 us
  transfers between devices with their start and end apart: 5, of which 2 were waited for; matrix products, arithmetic and copies ran while one was open for 0% of the time, Pallas kernels for 11%

profile of v4, /device:TPU:101, one launch (start us, length us, event | category | flops | bytes accessed | tf_op | source)
XLA Modules:
  0.0 30.6 jit_solution(16040664871609621563)
XLA Ops:
  0.0 1.3 %pack_x.1 = (bf16[544,128]{1,0:T(8,128)(2,1)S(1)}, bf16[544,128]{1,0:T(8,128)(2,1)S(1)}, bf16[1088,128]{1,0:T(8,128)(2,1)S(1)}, f32[2,16,32,128]{3,2,1,0:T(8,128...) custom-call(f32[2,16,32,128]{3,2,1,0:T(8,128)} %u_hbm.1, bf16[3,16,32,128]{3,2,1,0:T(8,128)(2,1)} %t_hbm.1, ...), custom_call_target="tpu_custom_call" | custom-call | tf_op jit(solution)/shard_map/pack_x/pallas_call | solution.py:147
  1.4 3.2 %collective-permute-start = (bf16[544,128]{1,0:T(8,128)(2,1)S(1)}, bf16[544,128]{1,0:T(8,128)(2,1)S(1)}, u32[]{:S(2)}, u32[]{:S(2)}) collective-permute-start(bf16[544,128]{1,0:T(8,128)(2,1)S(1)} %get-tuple-element.18), channel_id=1, source_target_pairs={{0,1},{1,0},{2,3},{3,2},{4,5},{5,4},{6,7},{7,6},{8,9},{9,8},{10,11... | collective-permute-start | bytes 417800 | tf_op jit(solution)/shard_map/ppermute | solution.py:23
  4.6 3.8 %collective-permute-start.1 = (bf16[544,128]{1,0:T(8,128)(2,1)S(1)}, bf16[544,128]{1,0:T(8,128)(2,1)S(1)}, u32[]{:S(2)}, u32[]{:S(2)}) collective-permute-start(bf16[544,128]{1,0:T(8,128)(2,1)S(1)} %get-tuple-element.19), channel_id=1, source_target_pairs={{1,2},{2,1},{3,4},{4,3},{5,6},{6,5},{7,8},{8,7},{9,10},{10,9},{11,... | collective-permute-start | bytes 417800 | tf_op jit(solution)/shard_map/ppermute | solution.py:23
  8.4 0.0 collective-permute-done.even_x_ref.even_ref
  8.4 4.5 %collective-permute-done.1.odd_x_ref.odd_ref = bf16[544,128]{1,0:T(8,128)(2,1)S(1)} collective-permute-done((bf16[544,128]{1,0:T(8,128)(2,1)S(1)}, bf16[544,128]{1,0:T(8,128)(2,1)S(1)}, u32[]{:S(2)}, u32[]{:S(2)}) %collective-permute-start.1) | collective-permute-done | bytes 139296 | tf_op jit(solution)/shard_map/ppermute | solution.py:23
  12.8 0.2 pack_z.1
  13.1 3.7 %collective-permute-start.2 = (bf16[1456,128]{1,0:T(8,128)(2,1)S(1)}, bf16[1456,128]{1,0:T(8,128)(2,1)S(1)}, u32[]{:S(2)}, u32[]{:S(2)}) collective-permute-start(bf16[1456,128]{1,0:T(8,128)(2,1)S(1)} %get-tuple-element.20), channel_id=1, source_target_pairs={{0,16},{16,0},{32,48},{48,32},{64,80},{80,64},{96,112},{112,96},{1... | collective-permute-start | bytes 1118216 | tf_op jit(solution)/shard_map/ppermute | solution.py:23
  16.8 4.7 %collective-permute-start.3 = (bf16[1088,128]{1,0:T(8,128)(2,1)S(1)}, bf16[1088,128]{1,0:T(8,128)(2,1)S(1)}, u32[]{:S(2)}, u32[]{:S(2)}) collective-permute-start(bf16[1088,128]{1,0:T(8,128)(2,1)S(1)} %get-tuple-element.24), channel_id=1, source_target_pairs={{16,32},{32,16},{48,64},{64,48},{80,96},{96,80},{112,128},{128,112... | collective-permute-start | bytes 835592 | tf_op jit(solution)/shard_map/ppermute | solution.py:23
  21.5 2.1 %collective-permute-start.4 = (bf16[368,128]{1,0:T(8,128)(2,1)S(1)}, bf16[368,128]{1,0:T(8,128)(2,1)S(1)}, u32[]{:S(2)}, u32[]{:S(2)}) collective-permute-start(bf16[368,128]{1,0:T(8,128)(2,1)S(1)} %get-tuple-element.25), channel_id=1, source_target_pairs={{16,32},{32,16},{48,64},{64,48},{80,96},{96,80},{112,128},{128,112... | collective-permute-start | bytes 282632 | tf_op jit(solution)/shard_map/ppermute | solution.py:23
  23.6 0.0 collective-permute-done.2.message_ref
  23.6 3.4 %sweep_far.1 = (f32[2,34,56,128]{3,2,1,0:T(8,128)S(1)}, f32[3,28,56,128]{3,2,1,0:T(8,128)S(1)}) custom-call(f32[2,16,32,128]{3,2,1,0:T(8,128)S(1)} %get-tuple-element.16.u.u0, bf16[3,16,32,128]{3,2,1,0:T(8,128)(2,1)S(1)} %get-tuple-element.17.t.t0, bf16[544,128]{1,0:T(8,128)(2,1)S(1)} %collective-permute-done.even_x_ref.even_ref, ...), custom_call_target="tpu_custom_call" | custom-call | flops 268435456 | bytes 16777216 | tf_op jit(solution)/shard_map/sweep_far/pallas_call | solution.py:384
  27.0 1.6 %collective-permute-done.4.corners_ref = bf16[368,128]{1,0:T(8,128)(2,1)S(1)} collective-permute-done((bf16[368,128]{1,0:T(8,128)(2,1)S(1)}, bf16[368,128]{1,0:T(8,128)(2,1)S(1)}, u32[]{:S(2)}, u32[]{:S(2)}) %collective-permute-start.4) | collective-permute-done | bytes 94240 | tf_op jit(solution)/shard_map/ppermute | solution.py:23
  28.6 0.0 collective-permute-done.3.message_ref
  28.6 2.0 %sweep_near.1 = (f32[2,16,32,128]{3,2,1,0:T(8,128)}, f32[2,34,56,128]{3,2,1,0:T(8,128)S(1)}, f32[3,28,56,128]{3,2,1,0:T(8,128)S(1)}) custom-call(f32[2,34,56,128]{3,2,1,0:T(8,128)S(1)} %get-tuple-element.22.u_in, f32[3,28,56,128]{3,2,1,0:T(8,128)S(1)} %get-tuple-element.23.t_in, ...), custom_call_target="tpu_custom_call", output_to_operand_aliasing={{1}: (0, {}), {2}: (1, {})} | custom-call | tf_op jit(solution)/shard_map/sweep_near/pallas_call | solution.py:430
Async XLA Ops:
  1.4 7.0 %collective-permute-start = (bf16[544,128]{1,0:T(8,128)(2,1)S(1)}, bf16[544,128]{1,0:T(8,128)(2,1)S(1)}, u32[]{:S(2)}, u32[]{:S(2)}) collective-permute-start(bf16[544,128]{1,0:T(8,128)(2,1)S(1)} %get-tuple-element.18), channel_id=1, source_target_pairs={{0,1},{1,0},{2,3},{3,2},{4,5},{5,4},{6,7},{7,6},{8,9},{9,8},{10,11... | collective-permute-start | bytes 417800 | tf_op jit(solution)/shard_map/ppermute | solution.py:23
  4.6 8.3 %collective-permute-start.1 = (bf16[544,128]{1,0:T(8,128)(2,1)S(1)}, bf16[544,128]{1,0:T(8,128)(2,1)S(1)}, u32[]{:S(2)}, u32[]{:S(2)}) collective-permute-start(bf16[544,128]{1,0:T(8,128)(2,1)S(1)} %get-tuple-element.19), channel_id=1, source_target_pairs={{1,2},{2,1},{3,4},{4,3},{5,6},{6,5},{7,8},{8,7},{9,10},{10,9},{11,... | collective-permute-start | bytes 417800 | tf_op jit(solution)/shard_map/ppermute | solution.py:23
  13.1 10.5 %collective-permute-start.2 = (bf16[1456,128]{1,0:T(8,128)(2,1)S(1)}, bf16[1456,128]{1,0:T(8,128)(2,1)S(1)}, u32[]{:S(2)}, u32[]{:S(2)}) collective-permute-start(bf16[1456,128]{1,0:T(8,128)(2,1)S(1)} %get-tuple-element.20), channel_id=1, source_target_pairs={{0,16},{16,0},{32,48},{48,32},{64,80},{80,64},{96,112},{112,96},{1... | collective-permute-start | bytes 1118216 | tf_op jit(solution)/shard_map/ppermute | solution.py:23
  16.8 11.8 %collective-permute-start.3 = (bf16[1088,128]{1,0:T(8,128)(2,1)S(1)}, bf16[1088,128]{1,0:T(8,128)(2,1)S(1)}, u32[]{:S(2)}, u32[]{:S(2)}) collective-permute-start(bf16[1088,128]{1,0:T(8,128)(2,1)S(1)} %get-tuple-element.24), channel_id=1, source_target_pairs={{16,32},{32,16},{48,64},{64,48},{80,96},{96,80},{112,128},{128,112... | collective-permute-start | bytes 835592 | tf_op jit(solution)/shard_map/ppermute | solution.py:23
  21.5 7.1 %collective-permute-start.4 = (bf16[368,128]{1,0:T(8,128)(2,1)S(1)}, bf16[368,128]{1,0:T(8,128)(2,1)S(1)}, u32[]{:S(2)}, u32[]{:S(2)}) collective-permute-start(bf16[368,128]{1,0:T(8,128)(2,1)S(1)} %get-tuple-element.25), channel_id=1, source_target_pairs={{16,32},{32,16},{48,64},{64,48},{80,96},{96,80},{112,128},{128,112... | collective-permute-start | bytes 282632 | tf_op jit(solution)/shard_map/ppermute | solution.py:23

commit v5 on v4

--- a/solution.py
+++ b/solution.py
@@ -287,7 +287,7 @@
 
 
 def advance(step, first, count, above, below, refs, inside_x, inside_in, beyond, nx):
-    u, t, g, data, _ = refs
+    u, t, g, _, _ = refs
     nv, nt = u.shape[0], u.shape[3]
     start, wide = (2, nx + 16) if step <= 2 else (4, nx + 8)
     window = slice(start, start + wide)
@@ -307,7 +307,6 @@
         upper = block.astype(BF16)
         lower = (block - upper.astype(F32)).astype(BF16)
         both = jnp.dot(jnp.concatenate([upper, lower], axis=1), g, preferred_element_type=F32)
-        data[0:rows, :] = both[:, 0:nt] + both[:, nt : 2 * nt]
         top = lax.broadcasted_iota(jnp.int32, (TILE, nt), 0) == 0
         if low == first:
             for cols in tiles:
@@ -332,7 +331,7 @@
                     carried[v] = turned
                     at = (v * (high - low) + e - low) * wide + cols.start - start
                     turn = (flux_in - before[v, cols.start]) + (flux_x - shifted)
-                    renewed = data[at : at + TILE, :] + turn
+                    renewed = (both[at : at + TILE, 0:nt] + both[at : at + TILE, nt : 2 * nt]) + turn
                     before[v, cols.start] = flux_in
                     if e >= beyond:
                         renewed = jnp.where(inside_in, renewed, 0.0)

time: 30.8 us -> 30.9 us (level)
  the two profiles are of different devices: /device:TPU:101 before, /device:TPU:231 now
where the time goes in v5:
time: 30.9 us; the launch traced here: 30.6 us
  starting transfers between devices  17.8 us (58%)
  Pallas kernels  6.93 us (22%)
  waiting for transfers between devices  5.85 us (19%)
    ppermute x5, starting transfers between devices, pairing(): return lax.ppermute(value, axis, pairs)  17.8 us
    ppermute x5, waiting for transfers between devices, pairing(): return lax.ppermute(value, axis, pairs)  5.85 us
    pallas_call x1, Pallas kernels, sweep_far(): pl.pallas_call(kernel, out_shape=(jax.ShapeDtypeStruct((nv, height + STEP...  3.31 us
    pallas_call x1, Pallas kernels, sweep_near(): pl.pallas_call(kernel, out_shape=(jax.ShapeDtypeStruct((nv, ni, nx, nt),...  2.04 us
    pallas_call x1, Pallas kernels, pack_x(): pl.pallas_call(kernel, out_shape=(out, out, jax.ShapeDtypeStruct((len(o_p...  1.35 us
  transfers between devices with their start and end apart: 5, of which 2 were waited for; matrix products, arithmetic and copies ran while one was open for 0% of the time, Pallas kernels for 11%

profile of v5, /device:TPU:231, one launch (start us, length us, event | category | flops | bytes accessed | tf_op | source)
XLA Modules:
  0.0 30.6 jit_solution(7549954962790121471)
XLA Ops:
  0.0 1.3 %pack_x.1 = (bf16[544,128]{1,0:T(8,128)(2,1)S(1)}, bf16[544,128]{1,0:T(8,128)(2,1)S(1)}, bf16[1088,128]{1,0:T(8,128)(2,1)S(1)}, f32[2,16,32,128]{3,2,1,0:T(8,128...) custom-call(f32[2,16,32,128]{3,2,1,0:T(8,128)} %u_hbm.1, bf16[3,16,32,128]{3,2,1,0:T(8,128)(2,1)} %t_hbm.1, ...), custom_call_target="tpu_custom_call" | custom-call | tf_op jit(solution)/shard_map/pack_x/pallas_call | solution.py:147
  1.4 3.2 %collective-permute-start = (bf16[544,128]{1,0:T(8,128)(2,1)S(1)}, bf16[544,128]{1,0:T(8,128)(2,1)S(1)}, u32[]{:S(2)}, u32[]{:S(2)}) collective-permute-start(bf16[544,128]{1,0:T(8,128)(2,1)S(1)} %get-tuple-element.18), channel_id=1, source_target_pairs={{0,1},{1,0},{2,3},{3,2},{4,5},{5,4},{6,7},{7,6},{8,9},{9,8},{10,11... | collective-permute-start | bytes 417800 | tf_op jit(solution)/shard_map/ppermute | solution.py:23
  4.6 4.1 %collective-permute-start.1 = (bf16[544,128]{1,0:T(8,128)(2,1)S(1)}, bf16[544,128]{1,0:T(8,128)(2,1)S(1)}, u32[]{:S(2)}, u32[]{:S(2)}) collective-permute-start(bf16[544,128]{1,0:T(8,128)(2,1)S(1)} %get-tuple-element.19), channel_id=1, source_target_pairs={{1,2},{2,1},{3,4},{4,3},{5,6},{6,5},{7,8},{8,7},{9,10},{10,9},{11,... | collective-permute-start | bytes 417800 | tf_op jit(solution)/shard_map/ppermute | solution.py:23
  8.7 0.0 collective-permute-done.even_x_ref.even_ref
  8.7 4.2 %collective-permute-done.1.odd_x_ref.odd_ref = bf16[544,128]{1,0:T(8,128)(2,1)S(1)} collective-permute-done((bf16[544,128]{1,0:T(8,128)(2,1)S(1)}, bf16[544,128]{1,0:T(8,128)(2,1)S(1)}, u32[]{:S(2)}, u32[]{:S(2)}) %collective-permute-start.1) | collective-permute-done | bytes 139296 | tf_op jit(solution)/shard_map/ppermute | solution.py:23
  12.8 0.2 pack_z.1
  13.1 3.7 %collective-permute-start.2 = (bf16[1456,128]{1,0:T(8,128)(2,1)S(1)}, bf16[1456,128]{1,0:T(8,128)(2,1)S(1)}, u32[]{:S(2)}, u32[]{:S(2)}) collective-permute-start(bf16[1456,128]{1,0:T(8,128)(2,1)S(1)} %get-tuple-element.20), channel_id=1, source_target_pairs={{0,16},{16,0},{32,48},{48,32},{64,80},{80,64},{96,112},{112,96},{1... | collective-permute-start | bytes 1118216 | tf_op jit(solution)/shard_map/ppermute | solution.py:23
  16.8 4.7 %collective-permute-start.3 = (bf16[1088,128]{1,0:T(8,128)(2,1)S(1)}, bf16[1088,128]{1,0:T(8,128)(2,1)S(1)}, u32[]{:S(2)}, u32[]{:S(2)}) collective-permute-start(bf16[1088,128]{1,0:T(8,128)(2,1)S(1)} %get-tuple-element.24), channel_id=1, source_target_pairs={{16,32},{32,16},{48,64},{64,48},{80,96},{96,80},{112,128},{128,112... | collective-permute-start | bytes 835592 | tf_op jit(solution)/shard_map/ppermute | solution.py:23
  21.5 2.1 %collective-permute-start.4 = (bf16[368,128]{1,0:T(8,128)(2,1)S(1)}, bf16[368,128]{1,0:T(8,128)(2,1)S(1)}, u32[]{:S(2)}, u32[]{:S(2)}) collective-permute-start(bf16[368,128]{1,0:T(8,128)(2,1)S(1)} %get-tuple-element.25), channel_id=1, source_target_pairs={{16,32},{32,16},{48,64},{64,48},{80,96},{96,80},{112,128},{128,112... | collective-permute-start | bytes 282632 | tf_op jit(solution)/shard_map/ppermute | solution.py:23
  23.6 0.0 collective-permute-done.2.message_ref
  23.6 3.3 %sweep_far.1 = (f32[2,34,56,128]{3,2,1,0:T(8,128)S(1)}, f32[3,28,56,128]{3,2,1,0:T(8,128)S(1)}) custom-call(f32[2,16,32,128]{3,2,1,0:T(8,128)S(1)} %get-tuple-element.16.u.u0, bf16[3,16,32,128]{3,2,1,0:T(8,128)(2,1)S(1)} %get-tuple-element.17.t.t0, bf16[544,128]{1,0:T(8,128)(2,1)S(1)} %collective-permute-done.even_x_ref.even_ref, ...), custom_call_target="tpu_custom_call" | custom-call | flops 268435456 | bytes 16777216 | tf_op jit(solution)/shard_map/sweep_far/pallas_call | solution.py:383
  26.9 1.7 %collective-permute-done.4.corners_ref = bf16[368,128]{1,0:T(8,128)(2,1)S(1)} collective-permute-done((bf16[368,128]{1,0:T(8,128)(2,1)S(1)}, bf16[368,128]{1,0:T(8,128)(2,1)S(1)}, u32[]{:S(2)}, u32[]{:S(2)}) %collective-permute-start.4) | collective-permute-done | bytes 94240 | tf_op jit(solution)/shard_map/ppermute | solution.py:23
  28.6 0.0 collective-permute-done.3.message_ref
  28.6 2.0 %sweep_near.1 = (f32[2,16,32,128]{3,2,1,0:T(8,128)}, f32[2,34,56,128]{3,2,1,0:T(8,128)S(1)}, f32[3,28,56,128]{3,2,1,0:T(8,128)S(1)}) custom-call(f32[2,34,56,128]{3,2,1,0:T(8,128)S(1)} %get-tuple-element.22.u_in, f32[3,28,56,128]{3,2,1,0:T(8,128)S(1)} %get-tuple-element.23.t_in, ...), custom_call_target="tpu_custom_call", output_to_operand_aliasing={{1}: (0, {}), {2}: (1, {})} | custom-call | tf_op jit(solution)/shard_map/sweep_near/pallas_call | solution.py:429
Async XLA Ops:
  1.4 7.3 %collective-permute-start = (bf16[544,128]{1,0:T(8,128)(2,1)S(1)}, bf16[544,128]{1,0:T(8,128)(2,1)S(1)}, u32[]{:S(2)}, u32[]{:S(2)}) collective-permute-start(bf16[544,128]{1,0:T(8,128)(2,1)S(1)} %get-tuple-element.18), channel_id=1, source_target_pairs={{0,1},{1,0},{2,3},{3,2},{4,5},{5,4},{6,7},{7,6},{8,9},{9,8},{10,11... | collective-permute-start | bytes 417800 | tf_op jit(solution)/shard_map/ppermute | solution.py:23
  4.6 8.3 %collective-permute-start.1 = (bf16[544,128]{1,0:T(8,128)(2,1)S(1)}, bf16[544,128]{1,0:T(8,128)(2,1)S(1)}, u32[]{:S(2)}, u32[]{:S(2)}) collective-permute-start(bf16[544,128]{1,0:T(8,128)(2,1)S(1)} %get-tuple-element.19), channel_id=1, source_target_pairs={{1,2},{2,1},{3,4},{4,3},{5,6},{6,5},{7,8},{8,7},{9,10},{10,9},{11,... | collective-permute-start | bytes 417800 | tf_op jit(solution)/shard_map/ppermute | solution.py:23
  13.1 10.5 %collective-permute-start.2 = (bf16[1456,128]{1,0:T(8,128)(2,1)S(1)}, bf16[1456,128]{1,0:T(8,128)(2,1)S(1)}, u32[]{:S(2)}, u32[]{:S(2)}) collective-permute-start(bf16[1456,128]{1,0:T(8,128)(2,1)S(1)} %get-tuple-element.20), channel_id=1, source_target_pairs={{0,16},{16,0},{32,48},{48,32},{64,80},{80,64},{96,112},{112,96},{1... | collective-permute-start | bytes 1118216 | tf_op jit(solution)/shard_map/ppermute | solution.py:23
  16.8 11.8 %collective-permute-start.3 = (bf16[1088,128]{1,0:T(8,128)(2,1)S(1)}, bf16[1088,128]{1,0:T(8,128)(2,1)S(1)}, u32[]{:S(2)}, u32[]{:S(2)}) collective-permute-start(bf16[1088,128]{1,0:T(8,128)(2,1)S(1)} %get-tuple-element.24), channel_id=1, source_target_pairs={{16,32},{32,16},{48,64},{64,48},{80,96},{96,80},{112,128},{128,112... | collective-permute-start | bytes 835592 | tf_op jit(solution)/shard_map/ppermute | solution.py:23
  21.5 7.1 %collective-permute-start.4 = (bf16[368,128]{1,0:T(8,128)(2,1)S(1)}, bf16[368,128]{1,0:T(8,128)(2,1)S(1)}, u32[]{:S(2)}, u32[]{:S(2)}) collective-permute-start(bf16[368,128]{1,0:T(8,128)(2,1)S(1)} %get-tuple-element.25), channel_id=1, source_target_pairs={{16,32},{32,16},{48,64},{64,48},{80,96},{96,80},{112,128},{128,112... | collective-permute-start | bytes 282632 | tf_op jit(solution)/shard_map/ppermute | solution.py:23
